TPU v7x, 32 devices: a whole 2x2x4 slice. The times are simulated.
32 devices in a mesh: grid: 8 (over z, x), chan: 4 (over y, core).
Axes of the slice: x: 2, y: 2, z: 4, core: 2. Of those that a mesh axis runs over, the one named last changes fastest.
Arguments:
- input_field: bfloat16 [256, 1024, 1024], P('chan', 'grid'), may hold values from -6 to 6
- out_cotangent: bfloat16 [256, 1024, 1024], P('chan', 'grid'), may hold values from -6 to 6
- core_first: float32 [256, 16], replicated, may hold values from -1.5 to 1.5
- core_second: float32 [16, 256, 16], replicated, may hold values from -1.5 to 1.5
- core_third: float32 [16, 128, 16], replicated, may hold values from -1.5 to 1.5
- column_mode_core: float32 [2, 16, 128], replicated, may hold values from -2 to 2
Outputs:
- output_field: bfloat16 [256, 1024, 1024], P('chan', 'grid')
- input_grad: bfloat16 [256, 1024, 1024], P('chan', 'grid')
- grad_first: float32 [256, 16], replicated
- grad_second: float32 [16, 256, 16], replicated
- grad_third: float32 [16, 128, 16], replicated
- grad_fourth: float32 [2, 16, 128], replicated
All inputs are finite; a program needn't handle non-finite values.
Results may differ from a plain program's by a relative error of at most 0.0079.
Values may be sent and summed in bfloat16 or wider, within the bound.
A program may use at most 128 MiB of HBM per device.

v0:
```python
import math

import jax
import jax.numpy as jnp
import numpy as np
from jax import lax
from jax.experimental import pallas as pl
from jax.experimental.pallas import tpu as pltpu
from jax.sharding import PartitionSpec as P

F32 = jnp.float32
BF16 = jnp.bfloat16
HI = lax.Precision.HIGHEST
STEP = 16


def params(mib=48):
    return pltpu.CompilerParams(vmem_limit_bytes=mib * 2**20)


def dot(a, b, precision=None):
    return jnp.dot(a, b, preferred_element_type=F32, precision=precision)


def dot_nt(a, b, precision=None):
    return lax.dot_general(
        a, b, (((1,), (1,)), ((), ())), preferred_element_type=F32, precision=precision
    )


def dot_tn(a, b, precision=None):
    return lax.dot_general(
        a, b, (((0,), (0,)), ((), ())), preferred_element_type=F32, precision=precision
    )


def width_table(side, modes_y):
    phase = np.arange(side)[:, None] * np.arange(modes_y)[None, :] % side
    angle = phase.astype(np.float32) * np.float32(2.0 * math.pi / side)
    return np.concatenate([np.cos(angle), -np.sin(angle)], axis=1).astype(BF16)


def turn_table(side, modes_x):
    kx = np.arange(modes_x)
    freq = np.where(kx < modes_x // 2, kx, side - modes_x + kx)
    phase = freq[:, None] * np.arange(side)[None, :] % side
    angle = phase.astype(np.float32) * np.float32(2.0 * math.pi / side)
    return np.stack([np.cos(angle), np.sin(angle)]).astype(BF16)


def forward_turn(cs, block):
    x = dot(cs, block)
    n, m = x.shape[0] // 2, x.shape[1] // 2
    return x[:n, :m] + x[n:, m:], x[:n, m:] - x[n:, :m]


def inverse_turn(cs, block):
    x = dot(cs, block)
    n, m = x.shape[0] // 2, x.shape[1] // 2
    return x[:n, :m] - x[n:, m:], x[:n, m:] + x[n:, :m]


def spread(values, rows):
    n = values.shape[1]
    lane = lax.broadcasted_iota(jnp.int32, (n, n * STEP), 1)
    row = lax.broadcasted_iota(jnp.int32, (n, n * STEP), 0)
    wide = dot(values, (lane // STEP == row).astype(BF16))
    at = lax.broadcasted_iota(jnp.int32, (STEP, n * STEP), 1) % STEP
    unit = (at == lax.broadcasted_iota(jnp.int32, (STEP, n * STEP), 0)).astype(F32)
    return (wide[:, None, :] * unit[None]).reshape(rows * STEP, n * STEP).astype(BF16)


def lead_kernel(first_t, table, cs, field, modes, lead, kron, rows):
    step = pl.program_id(0)
    chan, _, side = field.shape
    rank = first_t.shape[0]
    wide = table.shape[1]

    @pl.when(step == 0)
    def _():
        kron[...] = spread(first_t[...], rank)

    product = dot(field[...].reshape(chan * STEP, side), table[...]).astype(BF16)
    modes[...] = product.reshape(chan, STEP, wide)
    mixed = dot(kron[...], product)
    rows[:, pl.ds(pl.multiple_of(step * STEP, STEP), STEP), :] = mixed.reshape(
        rank, STEP, wide
    ).astype(BF16)

    @pl.when(step == pl.num_programs(0) - 1)
    def _():
        half = wide // 2
        for a in range(rank):
            re, im = forward_turn(cs[...], rows[a])
            lead[a, :, :half] = re * (1.0 / side)
            lead[a, :, half:] = im * (1.0 / side)


def grad_kernel(table, cs, weight, field, spectrum, held):
    chan, rows, side = field.shape
    wide = table.shape[1]
    half = wide // 2
    product = dot(field[...].reshape(chan * rows, side), table[...]).astype(BF16)
    for c in range(chan):
        re, im = forward_turn(cs[...], product[c * rows : (c + 1) * rows])
        held[c, :, :half] = re * weight[:, :half]
        held[c, :, half:] = im * weight[:, half:]
    spectrum[...] = jnp.swapaxes(held[...], 0, 1).astype(BF16)


def back_kernel(second_ba, kernel, spectrum, out, held):
    rank_b = kernel.shape[1]
    rank_a = second_ba.shape[0] // rank_b
    half = kernel.shape[2] // 2

    def body(k, carry):
        g = dot(second_ba[...], spectrum[k])
        kr = kernel[k]
        re = jnp.zeros((rank_a, half), F32)
        im = jnp.zeros((rank_a, half), F32)
        for b in range(rank_b):
            gre = g[b * rank_a : (b + 1) * rank_a, :half]
            gim = g[b * rank_a : (b + 1) * rank_a, half:]
            kre, kim = kr[b : b + 1, :half], kr[b : b + 1, half:]
            re += gre * kre + gim * kim
            im += gim * kre - gre * kim
        held[k, :, :half] = re
        held[k, :, half:] = im
        return carry

    lax.fori_loop(0, STEP, body, 0, unroll=2)
    out[...] = jnp.swapaxes(held[...], 0, 1)


def mix_kernel(
    lead, kernel, spectrum, second_ab, second_t, third, column,
    out, part_second, part_third, part_fourth,
    lead_k, outer, out_k, kernel_grad,
):
    rank_a = lead.shape[0]
    rank_b = kernel.shape[1]
    half = kernel.shape[2] // 2
    lead_k[...] = jnp.swapaxes(lead[...], 0, 1)

    @pl.when(pl.program_id(0) == 0)
    def _():
        part_second[...] = jnp.zeros_like(part_second)
        part_fourth[...] = jnp.zeros_like(part_fourth)

    def body(k, carry):
        spec = spectrum[k]
        g = dot(second_ab[...], spec)
        kr, ld = kernel[k], lead_k[k]
        kre, kim = kr[:, :half], kr[:, half:]
        re = jnp.zeros((rank_b, half), F32)
        im = jnp.zeros((rank_b, half), F32)
        for a in range(rank_a):
            rows = slice(a * rank_b, (a + 1) * rank_b)
            lre, lim = ld[a : a + 1, :half], ld[a : a + 1, half:]
            outer[rows, :half] = (kre * lre - kim * lim).astype(BF16)
            outer[rows, half:] = (kre * lim + kim * lre).astype(BF16)
            gre, gim = g[rows, :half], g[rows, half:]
            re += gre * lre + gim * lim
            im += gim * lre - gre * lim
        at = pl.ds(pl.multiple_of(k * rank_b, rank_b), rank_b)
        kernel_grad[at, :half] = re
        kernel_grad[at, half:] = im
        out_k[k] = dot(second_t[...], outer[...])
        part_second[...] += dot_nt(spec, outer[...])
        return carry

    lax.fori_loop(0, STEP, body, 0, unroll=2)
    out[...] = jnp.swapaxes(out_k[...], 0, 1).astype(BF16)
    part_third[0] = dot_nt(column[...], kernel_grad[...], HI)
    part_fourth[...] += dot_tn(third[...], kernel_grad[...], HI)


def field_kernel(cs, table, spectrum, out, rows):
    chan = spectrum.shape[0]
    n = out.shape[1]
    half = table.shape[0] // 2
    lane = lax.broadcasted_iota(jnp.int32, (n, half), 1)
    scale = jnp.where(lane == 0, 1.0, 2.0) * (1.0 / table.shape[1])
    for c in range(chan):
        re, im = inverse_turn(cs[...], spectrum[c])
        rows[c * n : (c + 1) * n, :half] = (re * scale).astype(BF16)
        rows[c * n : (c + 1) * n, half:] = (im * scale).astype(BF16)
        out[c] = dot(rows[c * n : (c + 1) * n, :], table[...]).astype(BF16)


def first_kernel(cs, lead_grad, modes, rows, part_first, total):
    step = pl.program_id(0)
    rank, n, wide = rows.shape
    chan = modes.shape[0]
    half = wide // 2

    @pl.when(step == 0)
    def _():
        total[...] = jnp.zeros_like(total)
        for a in range(rank):
            re, im = inverse_turn(cs[...], lead_grad[a].astype(BF16))
            rows[a, :, :half] = re.astype(BF16)
            rows[a, :, half:] = im.astype(BF16)

    at = pl.ds(pl.multiple_of(step * STEP, STEP), STEP)
    block = rows[:, at, :].reshape(rank * STEP, wide)
    total[...] += dot_nt(modes[...].reshape(chan * STEP, wide), block)

    @pl.when(step == pl.num_programs(0) - 1)
    def _():
        shape = (STEP, rank * STEP)
        unit = lax.broadcasted_iota(jnp.int32, shape, 1) % STEP == lax.broadcasted_iota(
            jnp.int32, shape, 0
        )
        kept = total[...].reshape(chan, STEP, rank * STEP) * unit.astype(F32)[None]
        lane = lax.broadcasted_iota(jnp.int32, (rank, rank * STEP), 1)
        row = lax.broadcasted_iota(jnp.int32, (rank, rank * STEP), 0)
        pick = (lane // STEP == row).astype(F32)
        part_first[...] = dot_nt(pick, jnp.sum(kept, axis=1), HI)


def input_kernel(first, table, rows, out, kron):
    rank, _, wide = rows.shape
    chan, _, side = out.shape

    @pl.when(pl.program_id(0) == 0)
    def _():
        kron[...] = spread(first[...], chan)

    block = dot(kron[...], rows[...].reshape(rank * STEP, wide)) * (1.0 / side)
    out[...] = dot(block.astype(BF16), table[...]).astype(BF16).reshape(out.shape)


def whole(shape):
    return pl.BlockSpec(shape, lambda i: (0,) * len(shape))


def halvings(order, units):
    start, size, plan = 0, units, []
    for axis, bit in order:
        size //= 2
        side = lax.axis_index(axis) // bit % 2
        plan.append((axis, bit, side, start + side * size, start + (1 - side) * size, size))
        start = start + side * size
    return plan


def partner(axis, bit, side):
    return {axis: lax.axis_index(axis) + bit * (1 - 2 * side)}


def reduce_kernel(orders, *refs):
    count = len(orders)
    inputs, outputs = refs[:count], refs[count : 2 * count]
    totals, landed = refs[2 * count : 3 * count], refs[3 * count : 4 * count]
    send_sem, recv_sem = refs[4 * count :]
    plans = [halvings(order, ref.shape[0]) for order, ref in zip(orders, inputs)]
    steps = len(orders[0])
    barrier = pltpu.get_barrier_semaphore()
    for axis, bit, side, *_ in plans[0]:
        pl.semaphore_signal(
            barrier, inc=1, device_id=partner(axis, bit, side),
            device_id_type=pl.DeviceIdType.MESH,
        )
    pl.semaphore_wait(barrier, steps)

    for step in range(steps):
        copies = []
        for c in range(count):
            axis, bit, side, _, other, size = plans[c][step]
            source = inputs[c] if step == 0 else totals[c]
            first = inputs[c].shape[0] - 2 * size
            copy = pltpu.make_async_remote_copy(
                src_ref=source.at[pl.ds(other, size)],
                dst_ref=landed[c].at[pl.ds(first, size)],
                send_sem=send_sem.at[0, c, step],
                recv_sem=recv_sem.at[0, c, step],
                device_id=partner(axis, bit, side),
                device_id_type=pl.DeviceIdType.MESH,
            )
            copy.start()
            copies.append(copy)
        for c in range(count):
            _, _, _, own, _, size = plans[c][step]
            source = inputs[c] if step == 0 else totals[c]
            target = outputs[c] if step == steps - 1 else totals[c]
            first = inputs[c].shape[0] - 2 * size
            copies[c].wait()
            target[pl.ds(own, size)] = source[pl.ds(own, size)] + landed[c][pl.ds(first, size)]

    for step in reversed(range(steps)):
        copies = []
        for c in range(count):
            axis, bit, side, own, _, size = plans[c][step]
            copy = pltpu.make_async_remote_copy(
                src_ref=outputs[c].at[pl.ds(own, size)],
                dst_ref=outputs[c].at[pl.ds(own, size)],
                send_sem=send_sem.at[1, c, step],
                recv_sem=recv_sem.at[1, c, step],
                device_id=partner(axis, bit, side),
                device_id_type=pl.DeviceIdType.MESH,
            )
            copy.start()
            copies.append(copy)
        for copy in copies:
            copy.wait()


def bits(axis):
    return [(axis, 1 << n) for n in range((lax.axis_size(axis) - 1).bit_length())]


def sum_all(arrays, collective_id):
    chan, grid = bits("chan"), bits("grid")
    orders = [chan + grid, chan[:1] + grid + chan[1:]][: len(arrays)]
    wide = arrays[0].shape[-1]
    flat = [a.reshape(-1, 8, wide) for a in arrays]
    vmem = pl.BlockSpec(memory_space=pltpu.VMEM)
    results = pl.pallas_call(
        lambda *refs: reduce_kernel(orders, *refs),
        in_specs=[vmem] * len(flat),
        out_specs=[vmem] * len(flat),
        out_shape=[jax.ShapeDtypeStruct(a.shape, F32) for a in flat],
        scratch_shapes=[pltpu.VMEM(a.shape, F32) for a in flat]
        + [pltpu.VMEM(a.shape, F32) for a in flat]
        + [pltpu.SemaphoreType.DMA((2, len(flat), len(orders[0])))] * 2,
        compiler_params=pltpu.CompilerParams(
            collective_id=collective_id, has_side_effects=True, vmem_limit_bytes=48 * 2**20
        ),
        name="sum_all",
    )(*flat)
    return [r.reshape(a.shape) for r, a in zip(results, arrays)]


def local(input_field, out_cotangent, core_first, core_second, core_third, column_mode_core):
    grid_count = lax.axis_size("grid")
    grid_index = lax.axis_index("grid")
    chan_index = lax.axis_index("chan")
    chan, rows, side = input_field.shape
    channels, rank_a = core_first.shape
    rank_b, modes_x, rank_d = core_third.shape
    modes_y = column_mode_core.shape[2]
    wide = 2 * modes_y

    table_np = width_table(side, modes_y)
    table = jnp.asarray(table_np)
    table_t = jnp.asarray(np.ascontiguousarray(table_np.T))
    turns = turn_table(side, modes_x).reshape(2, modes_x, grid_count, rows)
    forward = np.ascontiguousarray(turns.transpose(2, 0, 1, 3)).reshape(
        grid_count, 2 * modes_x, rows
    )
    backward = np.ascontiguousarray(turns.transpose(2, 0, 3, 1)).reshape(
        grid_count, 2 * rows, modes_x
    )
    cs = lax.dynamic_index_in_dim(jnp.asarray(forward), grid_index, 0, keepdims=False)
    cs_t = lax.dynamic_index_in_dim(jnp.asarray(backward), grid_index, 0, keepdims=False)
    weight_c = np.where(np.arange(wide) % modes_y == 0, 1.0, 2.0).astype(np.float32)
    weight = jnp.asarray((weight_c / side)[None, :])

    first_local = lax.dynamic_slice_in_dim(core_first, chan_index * chan, chan, 0)
    second_local = lax.dynamic_slice_in_dim(core_second, chan_index * chan, chan, 1)
    first_bf = first_local.astype(BF16)
    second_bf = second_local.astype(BF16)
    pairs = rank_a * rank_b
    second_ab = second_bf.transpose(0, 2, 1).reshape(pairs, chan)
    second_ba = second_bf.transpose(2, 0, 1).reshape(pairs, chan)
    second_t = second_bf.transpose(1, 0, 2).reshape(chan, pairs)
    third_rows = core_third.transpose(1, 0, 2).reshape(modes_x * rank_b, rank_d)
    column = column_mode_core.transpose(1, 0, 2).reshape(rank_d, wide)
    kernel = dot(third_rows, column, HI).reshape(modes_x, rank_b, wide)

    row_steps = rows // STEP
    mode_steps = modes_x // STEP
    chan_step = min(chan, STEP)
    out_step = min(chan, 8)

    row_modes, lead = pl.pallas_call(
        lead_kernel,
        grid=(row_steps,),
        in_specs=[
            whole((rank_a, chan)),
            whole((side, wide)),
            whole((2 * modes_x, rows)),
            pl.BlockSpec((chan, STEP, side), lambda i: (0, i, 0)),
        ],
        out_specs=[
            pl.BlockSpec((chan, STEP, wide), lambda i: (0, i, 0)),
            whole((rank_a, modes_x, wide)),
        ],
        out_shape=[
            jax.ShapeDtypeStruct((chan, rows, wide), BF16),
            jax.ShapeDtypeStruct((rank_a, modes_x, wide), F32),
        ],
        scratch_shapes=[
            pltpu.VMEM((rank_a * STEP, chan * STEP), BF16),
            pltpu.VMEM((rank_a, rows, wide), BF16),
        ],
        compiler_params=params(),
        name="lead",
    )(first_bf.T, table, cs, input_field)

    spec_grad = pl.pallas_call(
        grad_kernel,
        grid=(chan // chan_step,),
        in_specs=[
            whole((side, wide)),
            whole((2 * modes_x, rows)),
            whole((1, wide)),
            pl.BlockSpec((chan_step, rows, side), lambda i: (i, 0, 0)),
        ],
        out_specs=pl.BlockSpec((modes_x, chan_step, wide), lambda i: (0, i, 0)),
        out_shape=jax.ShapeDtypeStruct((modes_x, chan, wide), BF16),
        scratch_shapes=[pltpu.VMEM((chan_step, modes_x, wide), F32)],
        compiler_params=params(),
        name="spec_grad",
    )(table, cs, weight, out_cotangent)

    lead_grad = pl.pallas_call(
        back_kernel,
        grid=(mode_steps,),
        in_specs=[
            whole((pairs, chan)),
            pl.BlockSpec((STEP, rank_b, wide), lambda i: (i, 0, 0)),
            pl.BlockSpec((STEP, chan, wide), lambda i: (i, 0, 0)),
        ],
        out_specs=pl.BlockSpec((rank_a, STEP, wide), lambda i: (0, i, 0)),
        out_shape=jax.ShapeDtypeStruct((rank_a, modes_x, wide), F32),
        scratch_shapes=[pltpu.VMEM((STEP, rank_a, wide), F32)],
        compiler_params=params(),
        name="lead_grad",
    )(second_ba, kernel, spec_grad)
    lead, lead_grad = sum_all([lead, lead_grad], 0)

    spec_out, part_second, part_third, part_fourth = pl.pallas_call(
        mix_kernel,
        grid=(mode_steps,),
        in_specs=[
            pl.BlockSpec((rank_a, STEP, wide), lambda i: (0, i, 0)),
            pl.BlockSpec((STEP, rank_b, wide), lambda i: (i, 0, 0)),
            pl.BlockSpec((STEP, chan, wide), lambda i: (i, 0, 0)),
            whole((pairs, chan)),
            whole((chan, pairs)),
            pl.BlockSpec((STEP * rank_b, rank_d), lambda i: (i, 0)),
            whole((rank_d, wide)),
        ],
        out_specs=[
            pl.BlockSpec((chan, STEP, wide), lambda i: (0, i, 0)),
            whole((chan, pairs)),
            pl.BlockSpec((1, rank_d, STEP * rank_b), lambda i: (i, 0, 0)),
            whole((rank_d, wide)),
        ],
        out_shape=[
            jax.ShapeDtypeStruct((chan, modes_x, wide), BF16),
            jax.ShapeDtypeStruct((chan, pairs), F32),
            jax.ShapeDtypeStruct((mode_steps, rank_d, STEP * rank_b), F32),
            jax.ShapeDtypeStruct((rank_d, wide), F32),
        ],
        scratch_shapes=[
            pltpu.VMEM((STEP, rank_a, wide), F32),
            pltpu.VMEM((pairs, wide), BF16),
            pltpu.VMEM((STEP, chan, wide), F32),
            pltpu.VMEM((STEP * rank_b, wide), F32),
        ],
        compiler_params=params(),
        name="mix",
    )(lead, kernel, spec_grad, second_ab, second_t, third_rows, column)

    back_rows, part_first = pl.pallas_call(
        first_kernel,
        grid=(row_steps,),
        in_specs=[
            whole((2 * rows, modes_x)),
            whole((rank_a, modes_x, wide)),
            pl.BlockSpec((chan, STEP, wide), lambda i: (0, i, 0)),
        ],
        out_specs=[whole((rank_a, rows, wide)), whole((rank_a, chan))],
        out_shape=[
            jax.ShapeDtypeStruct((rank_a, rows, wide), BF16),
            jax.ShapeDtypeStruct((rank_a, chan), F32),
        ],
        scratch_shapes=[pltpu.VMEM((chan * STEP, rank_a * STEP), F32)],
        compiler_params=params(),
        name="first",
    )(cs_t, lead_grad, row_modes)

    first_wide = lax.dynamic_update_slice(
        jnp.zeros((rank_a, channels), F32), part_first * (1.0 / side), (0, chan_index * chan)
    )
    second_wide = lax.dynamic_update_slice(
        jnp.zeros((channels, pairs), F32), part_second, (chan_index * chan, 0)
    )
    sizes = [first_wide.size, second_wide.size, part_third.size, part_fourth.size]
    packed = jnp.concatenate(
        [v.reshape(-1, wide) for v in (first_wide, second_wide, part_third, part_fourth)]
    )
    block = 8 * grid_count * lax.axis_size("chan")
    packed = jnp.pad(packed, ((0, -packed.shape[0] % block), (0, 0)))
    packed = sum_all([packed], 1)[0] * (1.0 / modes_x)
    cuts = np.cumsum([0] + [s // wide for s in sizes])
    one, two, three, four = (packed[cuts[n] : cuts[n + 1]] for n in range(4))
    grad_first = one.reshape(rank_a, channels).T
    grad_second = two.reshape(channels, rank_a, rank_b).transpose(1, 0, 2)
    grad_third = (
        three.reshape(mode_steps, rank_d, STEP, rank_b)
        .transpose(3, 0, 2, 1)
        .reshape(rank_b, modes_x, rank_d)
    )
    grad_fourth = four.reshape(rank_d, 2, modes_y).transpose(1, 0, 2)

    output_field = pl.pallas_call(
        field_kernel,
        grid=(chan // out_step,),
        in_specs=[
            whole((2 * rows, modes_x)),
            whole((wide, side)),
            pl.BlockSpec((out_step, modes_x, wide), lambda i: (i, 0, 0)),
        ],
        out_specs=pl.BlockSpec((out_step, rows, side), lambda i: (i, 0, 0)),
        out_shape=jax.ShapeDtypeStruct((chan, rows, side), BF16),
        scratch_shapes=[pltpu.VMEM((out_step * rows, wide), BF16)],
        compiler_params=params(),
        name="output",
    )(cs_t, table_t, spec_out)

    input_grad = pl.pallas_call(
        input_kernel,
        grid=(row_steps,),
        in_specs=[
            whole((chan, rank_a)),
            whole((wide, side)),
            pl.BlockSpec((rank_a, STEP, wide), lambda i: (0, i, 0)),
        ],
        out_specs=pl.BlockSpec((chan, STEP, side), lambda i: (0, i, 0)),
        out_shape=jax.ShapeDtypeStruct((chan, rows, side), BF16),
        scratch_shapes=[pltpu.VMEM((chan * STEP, rank_a * STEP), BF16)],
        compiler_params=params(),
        name="input_grad",
    )(first_bf, table_t, back_rows)

    return output_field, input_grad, grad_first, grad_second, grad_third, grad_fourth


def solution(mesh):
    placed = (P("chan", "grid", None), P("chan", "grid", None), P(), P(), P(), P())
    return jax.shard_map(
        local,
        mesh=mesh,
        in_specs=placed,
        out_specs=(P("chan", "grid", None), P("chan", "grid", None), P(), P(), P(), P()),
        check_vma=False,
    )
```

profile of v0, /device:TPU:0, one launch (start us, length us, event | category | flops | bytes accessed | tf_op | source)
XLA Modules:
  0.0 238.5 jit_solution(7829702207497950569)
XLA Ops:
  0.7 0.8 constant_dynamic-slice_fusion
  1.7 0.7 copy.31
  2.5 0.7 copy_bitcast_fusion.column
  3.5 0.9 dynamic-slice_bitcast_fusion
  4.4 1.4 copy.33
  5.8 1.8 fusion.2.kernel
  7.6 13.8 %spec_grad.1.spectrum = bf16[128,64,256]{2,1,0:T(8,128)(2,1)S(1)} custom-call(bf16[1024,256]{1,0:T(8,128)(2,1)S(1)} %copy-done.5, bf16[256,128]{1,0:T(8,128)(2,1)S(1)} %get-tuple-element.34.cs, f32[1,256]{1,0:T(1,128)S(1)} %copy-done.8, bf16[64,128,1024]{2,1,0:T(8,128)(2,1)} %field.3), custom_call_target="tpu_custom_call" | custom-call | tf_op jit(solution)/shard_map/spec_grad/pallas_call | solution.py:402
  21.4 2.0 copy-done.2
  23.4 15.1 %lead_grad.1 = f32[16,128,256]{2,1,0:T(8,128)S(1)} custom-call(bf16[256,64]{1,0:T(8,128)(2,1)S(1)} %bitcast.51, f32[128,16,256]{2,1,0:T(8,128)S(1)} %fusion.2.kernel, bf16[128,64,256]{2,1,0:T(8,128)(2,1)} %copy-done.2), custom_call_target="tpu_custom_call" | custom-call | tf_op jit(solution)/shard_map/lead_grad/pallas_call | solution.py:418
  38.5 15.2 %lead.1 = (bf16[64,128,256]{2,1,0:T(8,128)(2,1)}, f32[16,128,256]{2,1,0:T(8,128)S(1)}) custom-call(bf16[16,64]{1,0:T(8,128)(2,1)S(1)} %copy.29.first_t, bf16[1024,256]{1,0:T(8,128)(2,1)S(1)} %copy-done.5, bf16[256,128]{1,0:T(8,128)(2,1)S(1)} %get-tuple-element.34.cs, bf16[64,128,1024]{2,1,0:T(8,128)(2,1)} %field.2), custom_call_target="tpu_custom_call" | custom-call | tf_op jit(solution)/shard_map/lead/pallas_call | solution.py:377
  53.7 1.3 copy-done.6
  55.0 75.7 %sum_all.2 = (f32[256,8,256]{2,1,0:T(8,128)S(1)}, f32[256,8,256]{2,1,0:T(8,128)S(1)}) custom-call(f32[256,8,256]{2,1,0:T(8,128)} %bitcast.47, f32[256,8,256]{2,1,0:T(8,128)} %bitcast.45), custom_call_target="tpu_custom_call" | custom-call | tf_op jit(solution)/shard_map/sum_all/pallas_call | solution.py:319
  130.7 27.8 %mix.1 = (bf16[64,128,256]{2,1,0:T(8,128)(2,1)}, f32[64,256]{1,0:T(8,128)S(1)}, f32[8,16,256]{2,1,0:T(8,128)S(1)}, f32[16,256]{1,0:T(8,128)S(1)}) custom-call(f32[16,128,256]{2,1,0:T(8,128)S(1)} %bitcast.48, f32[128,16,256]{2,1,0:T(8,128)S(1)} %fusion.2.kernel, bf16[128,64,256]{2,1,0:T(8,128)(2,1)} %copy-done.2, bf16[256,64]{1,0:T(8,128)(2,1)S(1)} %bitcast.50, ...), custom_call_target="tpu_custom_call" | custom-call | tf_op jit(solution)/shard_map/mix/pallas_call | solution.py:434
  158.6 7.1 %first.1 = (bf16[16,128,256]{2,1,0:T(8,128)(2,1)S(1)}, f32[16,64]{1,0:T(8,128)S(1)}) custom-call(bf16[256,128]{1,0:T(8,128)(2,1)S(1)} %get-tuple-element.35.cs, f32[16,128,256]{2,1,0:T(8,128)S(1)} %bitcast.46, bf16[64,128,256]{2,1,0:T(8,128)(2,1)} %get-tuple-element.20.modes), custom_call_target="tpu_custom_call" | custom-call | tf_op jit(solution)/shard_map/first/pallas_call | solution.py:468
  166.1 32.6 %sum_all.3 = f32[64,8,256]{2,1,0:T(8,128)S(1)} custom-call(f32[64,8,256]{2,1,0:T(8,128)S(1)} %fusion.refs_0_), custom_call_target="tpu_custom_call" | custom-call | tf_op jit(solution)/shard_map/sum_all/pallas_call | solution.py:319
  198.7 0.6 fusion.1
  199.3 0.6 copy.44
  200.3 1.7 copy.36
  202.1 2.2 reshape.83
  204.2 2.0 reshape.81
  206.2 3.2 %copy.38 = f32[16,256,16]{1,2,0:T(8,128)} copy(f32[16,256,16]{2,0,1:T(8,128)} %bitcast.54) | data formatting | bytes 524288
  209.4 2.2 copy-done.4
  211.6 17.1 %output.1 = bf16[64,128,1024]{2,1,0:T(8,128)(2,1)} custom-call(bf16[256,128]{1,0:T(8,128)(2,1)S(1)} %get-tuple-element.35.cs, bf16[256,1024]{1,0:T(8,128)(2,1)S(1)} %copy-done.7, bf16[64,128,256]{2,1,0:T(8,128)(2,1)S(1)} %copy-done.4), custom_call_target="tpu_custom_call" | custom-call | tf_op jit(solution)/shard_map/output/pallas_call | solution.py:510
  228.7 9.8 %input_grad.1 = bf16[64,128,1024]{2,1,0:T(8,128)(2,1)} custom-call(bf16[64,16]{1,0:T(8,128)(2,1)S(1)} %copy.40.first, bf16[256,1024]{1,0:T(8,128)(2,1)S(1)} %copy-done.7, bf16[16,128,256]{2,1,0:T(8,128)(2,1)S(1)} %get-tuple-element.21.rows), custom_call_target="tpu_custom_call" | custom-call | tf_op jit(solution)/shard_map/input_grad/pallas_call | solution.py:525
  (33 shorter events, 1.3 us)
Async XLA Ops:
  0.6 2.6 %copy-start = (f32[16,256,16]{1,2,0:T(8,128)S(1)}, f32[16,256,16]{1,2,0:T(8,128)}, u32[]{:S(2)}) copy-start(f32[16,256,16]{1,2,0:T(8,128)} %param.14) | copy-start | bytes 786436
  0.6 6.9 %copy-start.5 = (bf16[1024,256]{1,0:T(8,128)(2,1)S(1)}, bf16[1024,256]{1,0:T(8,128)(2,1)}, u32[]{:S(2)}) copy-start(bf16[1024,256]{1,0:T(8,128)(2,1)} %constant.40.clone.table) | copy-start | bytes 1572868
  0.7 6.9 %copy-start.8 = (f32[1,256]{1,0:T(1,128)S(1)}, f32[1,256]{1,0:T(1,128)}, u32[]{:S(2)}) copy-start(f32[1,256]{1,0:T(1,128)} %constant.44.clone.weight) | copy-start | bytes 3076
  21.4 2.0 copy-start.2
  38.5 15.2 %copy-start.3 = (f32[16,128,256]{2,1,0:T(8,128)}, f32[16,128,256]{2,1,0:T(8,128)S(1)}, u32[]{:S(2)}) copy-start(f32[16,128,256]{2,1,0:T(8,128)S(1)} %lead_grad.1) | copy-start | bytes 6291460
  53.7 1.3 copy-start.6
  200.3 9.1 %copy-start.7 = (bf16[256,1024]{1,0:T(8,128)(2,1)S(1)}, bf16[256,1024]{1,0:T(8,128)(2,1)}, u32[]{:S(2)}) copy-start(bf16[256,1024]{1,0:T(8,128)(2,1)} %constant.41.clone.table) | copy-start | bytes 1572868
  209.4 2.2 copy-start.4
  228.7 9.8 %copy-start.1 = (f32[16,256,16]{1,2,0:T(8,128)S(1)}, f32[16,256,16]{1,2,0:T(8,128)}, u32[]{:S(2)}) copy-start(f32[16,256,16]{1,2,0:T(8,128)} %param.14) | copy-start | bytes 786436
where the time goes:
time: 239 us
  Pallas kernels  214 us (90%)
  local copies, waits for them, and re-layouts  21.6 us (9%)
    pallas_call x2, Pallas kernels, sum_all(): pl.pallas_call(lambda *refs: reduce_kernel(orders, *refs), in_specs=[vmem...  108 us
    pallas_call x1, Pallas kernels, local(): pl.pallas_call(mix_kernel, grid=(mode_steps,), in_specs=[pl.BlockSpec((ra...  27.8 us
    pallas_call x1, Pallas kernels, local(): pl.pallas_call(field_kernel, grid=(chan // out_step,), in_specs=[whole((2...  17.1 us
    pallas_call x1, Pallas kernels, local(): pl.pallas_call(lead_kernel, grid=(row_steps,), in_specs=[whole((rank_a, c...  15.2 us
    pallas_call x1, Pallas kernels, local(): pl.pallas_call(back_kernel, grid=(mode_steps,), in_specs=[whole((pairs, c...  15.1 us
    pallas_call x1, Pallas kernels, local(): pl.pallas_call(grad_kernel, grid=(chan // chan_step,), in_specs=[whole((s...  13.8 us
    pallas_call x1, Pallas kernels, local(): pl.pallas_call(input_kernel, grid=(row_steps,), in_specs=[whole((chan, ra...  9.82 us
    unnamed x20, local copies, waits for them, and re-layouts  8.86 us

commit v1 on v0

v1 whole, which is shorter than its diff:
```python
import math

import jax
import jax.numpy as jnp
import numpy as np
from jax import lax
from jax.experimental import pallas as pl
from jax.experimental.pallas import tpu as pltpu
from jax.sharding import PartitionSpec as P

F32 = jnp.float32
BF16 = jnp.bfloat16
HI = lax.Precision.HIGHEST
STEP = 16
LANES = 128
MESH = pl.DeviceIdType.MESH


def params(mib=48):
    return pltpu.CompilerParams(vmem_limit_bytes=mib * 2**20)


def dot(a, b, precision=None):
    return jnp.dot(a, b, preferred_element_type=F32, precision=precision)


def dot_nt(a, b, precision=None):
    return lax.dot_general(
        a, b, (((1,), (1,)), ((), ())), preferred_element_type=F32, precision=precision
    )


def dot_tn(a, b, precision=None):
    return lax.dot_general(
        a, b, (((0,), (0,)), ((), ())), preferred_element_type=F32, precision=precision
    )


def width_table(side, modes_y):
    phase = np.arange(side)[:, None] * np.arange(modes_y)[None, :] % side
    angle = phase.astype(np.float32) * np.float32(2.0 * math.pi / side)
    return np.concatenate([np.cos(angle), -np.sin(angle)], axis=1).astype(BF16)


def turn_table(side, modes_x):
    kx = np.arange(modes_x)
    freq = np.where(kx < modes_x // 2, kx, side - modes_x + kx)
    phase = freq[:, None] * np.arange(side)[None, :] % side
    angle = phase.astype(np.float32) * np.float32(2.0 * math.pi / side)
    return np.stack([np.cos(angle), np.sin(angle)]).astype(BF16)


def spread(values, rows):
    n = values.shape[1]
    lane = lax.broadcasted_iota(jnp.int32, (n, n * STEP), 1)
    row = lax.broadcasted_iota(jnp.int32, (n, n * STEP), 0)
    wide = dot(values, (lane // STEP == row).astype(BF16))
    at = lax.broadcasted_iota(jnp.int32, (STEP, n * STEP), 1) % STEP
    unit = (at == lax.broadcasted_iota(jnp.int32, (STEP, n * STEP), 0)).astype(F32)
    return (wide[:, None, :] * unit[None]).reshape(rows * STEP, n * STEP).astype(BF16)


def lead_kernel(first_t, table, cs, field, modes, lead, csf, csb, kron, pairs, held):
    step = pl.program_id(0)
    chan, _, side = field.shape
    rank = first_t.shape[0]
    wide = table.shape[1]
    my = wide // 2
    mx, n = cs.shape[1:]

    @pl.when(step == 0)
    def _():
        kron[...] = spread(first_t[...], rank)
        c, s = cs[0], cs[1]
        csf[:mx, :n], csf[:mx, n:], csf[mx:, :n], csf[mx:, n:] = c, s, -s, c
        ct = jnp.swapaxes(c.astype(F32), 0, 1).astype(BF16)
        st = jnp.swapaxes(s.astype(F32), 0, 1).astype(BF16)
        csb[:n, :mx], csb[:n, mx:], csb[n:, :mx], csb[n:, mx:] = ct, -st, st, ct

    product = dot(field[...].reshape(chan * STEP, side), table[...]).astype(BF16)
    modes[...] = product.reshape(chan, STEP, wide)
    mixed = dot(kron[...], product).astype(BF16)
    for a in range(rank):
        for q in range(2):
            at = pl.ds(pl.multiple_of(q * n + step * STEP, STEP), STEP)
            pairs[a // 2, at, a % 2 * my : (a % 2 + 1) * my] = mixed[
                a * STEP : (a + 1) * STEP, q * my : (q + 1) * my
            ]

    @pl.when(step == pl.num_programs(0) - 1)
    def _():
        for p in range(rank // 2):
            z = dot(csf[...], pairs[p]) * (1.0 / side)
            held[2 * p] = z[:, :my]
            held[2 * p + 1] = z[:, my:]
        turned = jnp.swapaxes(held[...], 0, 1).astype(BF16)
        lead[:, 0] = turned[:mx]
        lead[:, 1] = turned[mx:]


def flip(index, bits):
    bit = 1
    while bit <= bits:
        if bits & bit:
            index = index + bit * (1 - 2 * (index // bit % 2))
        bit *= 2
    return index


class Place:
    def __init__(self):
        self.grid, self.chan = lax.axis_index("grid"), lax.axis_index("chan")
        self.core = self.chan % 2
        self.planes = lax.axis_size("chan")
        self.stacks = lax.axis_size("grid") // 2
        self.plane = self.chan // 2 * 2 + self.grid % 2
        self.stack = self.grid // 2

    def across_core(self):
        return {"grid": self.grid, "chan": flip(self.chan, 1)}

    def across_plane(self, s):
        return {"grid": flip(self.grid, s % 2), "chan": flip(self.chan, s // 2 * 2)}

    def across_stack(self, s):
        return {"grid": flip(self.grid, s * 2), "chan": self.chan}

    def peers(self):
        return (
            [self.across_core()]
            + [self.across_plane(s) for s in range(1, self.planes)]
            + [self.across_stack(s) for s in range(1, self.stacks)]
        )


def remote(src, dst, send, recv, peer):
    return pltpu.make_async_remote_copy(
        src_ref=src, dst_ref=dst, send_sem=send, recv_sem=recv,
        device_id=peer, device_id_type=MESH,
    )


class Reduce:
    def __init__(self, place, source, result, land_plane, land_stack, mid, send, recv):
        self.at, self.source, self.result = place, source, result
        self.land_plane, self.land_stack, self.mid = land_plane, land_stack, mid
        self.send, self.recv = send, recv
        self.chunk = source.shape[0] // place.planes
        self.piece = self.chunk // place.stacks

    def plane_copy(self, s):
        there = flip(self.at.plane, s)
        return remote(
            self.source.at[pl.ds(there * self.chunk, self.chunk)],
            self.land_plane.at[s - 1],
            self.send.at[0, s - 1], self.recv.at[0, s - 1], self.at.across_plane(s),
        )

    def plane_send(self):
        for s in range(1, self.at.planes):
            self.plane_copy(s).start()

    def plane_wait(self):
        for s in range(1, self.at.planes):
            self.plane_copy(s).wait()
        total = self.source[pl.ds(self.at.plane * self.chunk, self.chunk)].astype(F32)
        for s in range(1, self.at.planes):
            total = total + self.land_plane[s - 1].astype(F32)
        self.mid[...] = total.astype(self.mid.dtype)

    def stack_copy(self, s):
        there = flip(self.at.stack, s)
        return remote(
            self.mid.at[pl.ds(there * self.piece, self.piece)],
            self.land_stack.at[s - 1],
            self.send.at[1, s - 1], self.recv.at[1, s - 1], self.at.across_stack(s),
        )

    def stack_send(self):
        for s in range(1, self.at.stacks):
            self.stack_copy(s).start()

    def own(self):
        return pl.ds(self.at.plane * self.chunk + self.at.stack * self.piece, self.piece)

    def stack_wait(self):
        for s in range(1, self.at.stacks):
            self.stack_copy(s).wait()
        total = self.mid[pl.ds(self.at.stack * self.piece, self.piece)].astype(F32)
        for s in range(1, self.at.stacks):
            total = total + self.land_stack[s - 1].astype(F32)
        self.result[self.own()] = total.astype(self.result.dtype)

    def stack_back_copy(self, s):
        return remote(
            self.result.at[self.own()], self.result.at[self.own()],
            self.send.at[2, s - 1], self.recv.at[2, s - 1], self.at.across_stack(s),
        )

    def stack_back_send(self):
        for s in range(1, self.at.stacks):
            self.stack_back_copy(s).start()

    def stack_back_wait(self):
        for s in range(1, self.at.stacks):
            self.stack_back_copy(s).wait()

    def plane_back_copy(self, s):
        here = pl.ds(self.at.plane * self.chunk, self.chunk)
        return remote(
            self.result.at[here], self.result.at[here],
            self.send.at[3, s - 1], self.recv.at[3, s - 1], self.at.across_plane(s),
        )

    def plane_back_send(self):
        for s in range(1, self.at.planes):
            self.plane_back_copy(s).start()

    def plane_back_wait(self):
        for s in range(1, self.at.planes):
            self.plane_back_copy(s).wait()


def spectral_kernel(
    cot, modes_in, lead, csf, csb, table, second, third, column,
    rows_out, back_rows, g_first, g_second, g_third, g_fourth,
    cot_v, modes_v, rows_v, y, held, spec_stage, spec, s_stage, spec_out,
    by_ab, by_ba, by_t, kern, lead_f, kgrad, outer, held_o, part_second, back_in, total,
    lead_core, lead_x, lead_res, lead_lp, lead_ls, lead_mid,
    lg_x, lg_all, lg_lp, lg_ls, lg_mid,
    gp_core, gp_x, gp_all, gp_lp, gp_ls, gp_mid,
    f_core, f_plane, f_stack,
    lead_send, lead_recv, lg_send, lg_recv, gp_send, gp_recv,
    core_send, core_recv, spec_send, spec_recv, out_send, out_recv, f_send, f_recv,
    cot_sem, modes_sem, rows_sem,
):
    at = Place()
    core = at.core
    other = 1 - core
    chan, n, side = cot.shape
    wide = table.shape[1]
    my = wide // 2
    mx = lead.shape[0]
    half = mx // 2
    ra, rb, rd = lead.shape[2], third.shape[0], third.shape[1]
    pairs = ra * rb
    both = second.shape[1]
    channels = g_first.shape[1]
    sub = cot_v.shape[1]
    slots = cot_v.shape[0]
    subs = chan // sub
    lane = lax.broadcasted_iota(jnp.int32, (1, wide), 1)
    weight = jnp.where(lane % my == 0, 1.0, 2.0) * (1.0 / side)
    partner = at.across_core()

    def cot_copy(j):
        return pltpu.make_async_copy(
            cot.at[pl.ds(j * sub, sub)], cot_v.at[lax.rem(j, slots)], cot_sem.at[lax.rem(j, slots)]
        )

    modes_copy = pltpu.make_async_copy(modes_in, modes_v, modes_sem)

    barrier = pltpu.get_barrier_semaphore()
    peers = at.peers()
    for peer in peers:
        pl.semaphore_signal(barrier, inc=1, device_id=peer, device_id_type=MESH)
    for j in range(slots):
        cot_copy(j).start()
    modes_copy.start()

    sec = second[...]
    by_ab[...] = sec.astype(BF16)
    by_ba[...] = jnp.swapaxes(sec.reshape(ra, rb, both), 0, 1).reshape(pairs, both).astype(BF16)
    by_t[...] = jnp.swapaxes(sec, 0, 1).astype(BF16)
    col = jnp.concatenate([column[0], column[1]], axis=1)
    for b in range(rb):
        kgrad[b * half : (b + 1) * half, :] = dot_tn(third[b], col, HI)
    kern[...] = jnp.swapaxes(kgrad[...].reshape(rb, half, wide), 0, 1)

    lead_sum = Reduce(at, lead_x, lead_res, lead_lp, lead_ls, lead_mid, lead_send, lead_recv)
    lg_sum = Reduce(at, lg_x, lg_all.at[core], lg_lp, lg_ls, lg_mid, lg_send, lg_recv)
    gp_sum = Reduce(at, gp_x, gp_all.at[core], gp_lp, gp_ls, gp_mid, gp_send, gp_recv)

    def lead_core_copy():
        return remote(
            lead.at[pl.ds(other * half, half)], lead_core, core_send.at[0], core_recv.at[0], partner
        )

    pl.semaphore_wait(barrier, len(peers))
    lead_core_copy().start()

    def lead_start():
        lead_core_copy().wait()
        mine = lead[pl.ds(core * half, half)].astype(F32) + lead_core[...].astype(F32)
        lead_x[...] = mine.reshape(lead_x.shape).astype(BF16)
        lead_sum.plane_send()

    def spec_copy(i):
        return remote(
            spec_stage.at[i, pl.ds(other * half, half)],
            spec.at[:, pl.ds(core * chan + i * STEP, STEP), :],
            spec_send.at[i], spec_recv.at[i], partner,
        )

    def cot_body(i, carry):
        for s in range(STEP // sub):
            j = i * (STEP // sub) + s
            cot_copy(j).wait()
            block = cot_v[lax.rem(j, slots)].reshape(sub * n, side)
            product = dot(block, table[...]).astype(BF16)

            @pl.when(j + slots < subs)
            def _():
                cot_copy(j + slots).start()

            for c in range(sub):
                for q in range(2):
                    y[c // 2, q * n : (q + 1) * n, c % 2 * my : (c % 2 + 1) * my] = product[
                        c * n : (c + 1) * n, q * my : (q + 1) * my
                    ]
            for p in range(sub // 2):
                z = dot(csf[...], y[p]) * weight
                held[s * sub + 2 * p] = z[:, :my]
                held[s * sub + 2 * p + 1] = z[:, my:]
        turned = jnp.swapaxes(held[...], 0, 1).astype(BF16)
        spec_stage[i, :, :, :my] = turned[:mx]
        spec_stage[i, :, :, my:] = turned[mx:]
        spec_copy(i).start()
        spec[:, pl.ds(pl.multiple_of(core * chan + i * STEP, STEP), STEP), :] = spec_stage[
            i, pl.ds(core * half, half)
        ]

        @pl.when(i == 0)
        def _():
            lead_start()

        return carry

    lax.fori_loop(0, chan // STEP, cot_body, 0)
    lead_sum.plane_wait()
    lead_sum.stack_send()
    for i in range(chan // STEP):
        spec_copy(i).wait()

    unroll = 4

    def back_body(j, carry):
        for u in range(unroll):
            k = j * unroll + u
            g = dot(by_ba[...], spec[k])
            re = jnp.zeros((ra, my), F32)
            im = jnp.zeros((ra, my), F32)
            for b in range(rb):
                gre = g[b * ra : (b + 1) * ra, :my]
                gim = g[b * ra : (b + 1) * ra, my:]
                kre, kim = kern[k, b : b + 1, :my], kern[k, b : b + 1, my:]
                re += gre * kre + gim * kim
                im += gim * kre - gre * kim
            lg_x[2 * k] = re.astype(BF16)
            lg_x[2 * k + 1] = im.astype(BF16)
        return carry

    lax.fori_loop(0, half // unroll, back_body, 0)
    lg_sum.plane_send()
    lead_sum.stack_wait()
    lead_sum.stack_back_send()
    lead_sum.stack_back_wait()
    lead_sum.plane_back_send()
    lg_sum.plane_wait()
    lg_sum.stack_send()
    lead_sum.plane_back_wait()
    whole_lead = lead_res[...].reshape(half, 2, ra, my).astype(F32)
    lead_f[:, :, :my] = whole_lead[:, 0]
    lead_f[:, :, my:] = whole_lead[:, 1]
    part_second[...] = jnp.zeros_like(part_second)

    def out_copy(g):
        return remote(
            s_stage.at[g, pl.ds(other * (chan // 2), chan // 2)],
            spec_out.at[:, :, pl.ds(core * half + g * STEP, STEP), :],
            out_send.at[g], out_recv.at[g], partner,
        )

    per = 2

    def mix_body(j, carry):
        for u in range(per):
            k = j * per + u
            g = dot(by_ab[...], spec[k])
            kr = kern[k]
            kre, kim = kr[:, :my], kr[:, my:]
            re = jnp.zeros((rb, my), F32)
            im = jnp.zeros((rb, my), F32)
            for a in range(ra):
                rows = slice(a * rb, (a + 1) * rb)
                lre, lim = lead_f[k, a : a + 1, :my], lead_f[k, a : a + 1, my:]
                outer[rows, u * wide : u * wide + my] = (kre * lre - kim * lim).astype(BF16)
                outer[rows, u * wide + my : (u + 1) * wide] = (kre * lim + kim * lre).astype(BF16)
                gre, gim = g[rows, :my], g[rows, my:]
                re += gre * lre + gim * lim
                im += gim * lre - gre * lim
            at_k = pl.ds(pl.multiple_of(k * rb, rb), rb)
            kgrad[at_k, :my] = re
            kgrad[at_k, my:] = im
        for u in range(per):
            k = j * per + u
            held_o[lax.rem(k, STEP)] = dot(by_t[...], outer[:, u * wide : (u + 1) * wide])
        rhs = jnp.concatenate([spec[j * per + u] for u in range(per)], axis=1)
        part_second[...] += dot_nt(outer[...], rhs)
        return carry

    def mix_group(g, carry):
        lax.fori_loop(g * (STEP // per), (g + 1) * (STEP // per), mix_body, 0)
        turned = jnp.swapaxes(held_o[...], 0, 1).astype(BF16)
        turned = turned.reshape(both // 2, 2, STEP, wide)
        for c in range(2):
            for q in range(2):
                s_stage[g, :, q, :, c * my : (c + 1) * my] = turned[
                    :, c, :, q * my : (q + 1) * my
                ]
        out_copy(g).start()
        row = pl.ds(pl.multiple_of(core * half + g * STEP, STEP), STEP)
        spec_out[:, :, row, :] = s_stage[g, pl.ds(core * (chan // 2), chan // 2)]

        @pl.when(g == 1)
        def _():
            lg_sum.stack_wait()
            lg_sum.stack_back_send()

        @pl.when(g == 2)
        def _():
            lg_sum.stack_back_wait()
            lg_sum.plane_back_send()

        return carry

    groups = half // STEP
    lax.fori_loop(0, groups, mix_group, 0)

    def second_copy():
        return remote(
            part_second.at[pl.ds(other * (pairs // 2), pairs // 2)], gp_core,
            core_send.at[1], core_recv.at[1], partner,
        )

    def back_copy():
        return remote(lg_all.at[core], lg_all.at[core], core_send.at[2], core_recv.at[2], partner)

    second_copy().start()
    lg_sum.plane_back_wait()
    back_copy().start()
    by_mode = jnp.swapaxes(kgrad[...].reshape(half, rb, wide), 0, 1).reshape(rb * half, wide)
    part_third = dot_nt(col, by_mode, HI)
    third_flat = jnp.concatenate([third[b] for b in range(rb)], axis=1)
    part_fourth = dot(third_flat, by_mode, HI)
    second_copy().wait()
    mine = part_second[pl.ds(core * (pairs // 2), pairs // 2)] + gp_core[...]
    lane_c = lax.broadcasted_iota(jnp.int32, (both, channels), 1)
    row_c = lax.broadcasted_iota(jnp.int32, (both, channels), 0)
    mine = dot(mine, (lane_c == row_c + at.chan // 2 * both).astype(F32), HI)

    pieces = []
    for value in (mine, part_third, part_fourth):
        for c in range(value.shape[1] // LANES):
            pieces.append((value, c))
    spots, count = [], 0
    for value, c in pieces:
        tiles = value.shape[0] // 8
        gp_x[count : count + tiles] = value[:, c * LANES : (c + 1) * LANES].reshape(
            tiles, 8, LANES
        )
        spots.append((count, tiles))
        count += tiles
    if count < gp_x.shape[0]:
        gp_x[count:] = jnp.zeros((gp_x.shape[0] - count, 8, LANES), F32)
    gp_sum.plane_send()

    back_copy().wait()
    for q in range(2):
        for h in range(2):
            got = lg_all[h].reshape(half, 2, ra, my)[:, q].astype(F32)
            turned = jnp.swapaxes(got, 0, 1).astype(BF16)
            for a in range(ra):
                back_in[
                    a // 2, q * mx + h * half : q * mx + (h + 1) * half,
                    a % 2 * my : (a % 2 + 1) * my,
                ] = turned[a]
    for p in range(ra // 2):
        r = dot(csb[...], back_in[p]).astype(BF16)
        for c in range(2):
            for q in range(2):
                back_rows[2 * p + c, :, q * my : (q + 1) * my] = r[
                    q * n : (q + 1) * n, c * my : (c + 1) * my
                ]
    modes_copy.wait()
    total[...] = jnp.zeros_like(total)

    def first_body(i, carry):
        row = pl.ds(pl.multiple_of(i * STEP, STEP), STEP)
        block = back_rows[:, row, :].reshape(ra * STEP, wide)
        total[...] += dot_nt(modes_v[:, row, :].reshape(chan * STEP, wide), block)
        return carry

    lax.fori_loop(0, n // STEP, first_body, 0)
    gp_sum.plane_wait()
    gp_sum.stack_send()
    shape = (STEP, ra * STEP)
    unit = lax.broadcasted_iota(jnp.int32, shape, 1) % STEP == lax.broadcasted_iota(
        jnp.int32, shape, 0
    )
    kept = total[...].reshape(chan, STEP, ra * STEP) * unit.astype(F32)[None]
    lane_f = lax.broadcasted_iota(jnp.int32, (ra, ra * STEP), 1)
    row_f = lax.broadcasted_iota(jnp.int32, (ra, ra * STEP), 0)
    pick = (lane_f // STEP == row_f).astype(F32)
    part_first = dot_nt(pick, jnp.sum(kept, axis=1), HI)
    lane_f = lax.broadcasted_iota(jnp.int32, (chan, channels), 1)
    row_f = lax.broadcasted_iota(jnp.int32, (chan, channels), 0)
    place_f = (lane_f == row_f + at.chan * chan).astype(F32)
    f_core[core] = dot(part_first, place_f, HI)

    def first_core_copy():
        return remote(f_core.at[core], f_core.at[core], core_send.at[3], core_recv.at[3], partner)

    def first_plane_copy(s):
        return remote(
            f_plane.at[at.plane], f_plane.at[at.plane],
            f_send.at[0, s - 1], f_recv.at[0, s - 1], at.across_plane(s),
        )

    def first_stack_copy(s):
        return remote(
            f_stack.at[at.stack], f_stack.at[at.stack],
            f_send.at[1, s - 1], f_recv.at[1, s - 1], at.across_stack(s),
        )

    def first_plane():
        first_core_copy().wait()
        f_plane[at.plane] = f_core[0] + f_core[1]
        for s in range(1, at.planes):
            first_plane_copy(s).start()

    def first_stack():
        for s in range(1, at.planes):
            first_plane_copy(s).wait()
        value = f_plane[0]
        for s in range(1, at.planes):
            value = value + f_plane[s]
        f_stack[at.stack] = value
        for s in range(1, at.stacks):
            first_stack_copy(s).start()

    first_core_copy().start()
    for g in range(groups):
        out_copy(g).wait()

    turns = 4

    def rows_copy(i):
        where = pl.ds(i * 2 * turns, 2 * turns)
        return pltpu.make_async_copy(rows_v.at[where], rows_out.at[where], rows_sem.at[i])

    def rows_body(i, carry):
        for t in range(turns):
            p = i * turns + t
            r = (dot(csb[...], spec_out[p].reshape(2 * mx, wide)) * weight).astype(BF16)
            for c in range(2):
                for q in range(2):
                    rows_v[2 * p + c, :, q * my : (q + 1) * my] = r[
                        q * n : (q + 1) * n, c * my : (c + 1) * my
                    ]
        rows_copy(i).start()

        @pl.when(i == 0)
        def _():
            first_plane()

        return carry

    steps = chan // 2 // turns
    lax.fori_loop(0, steps, rows_body, 0)
    first_stack()
    gp_sum.stack_wait()
    gp_sum.stack_back_send()
    gp_sum.stack_back_wait()
    gp_sum.plane_back_send()
    for s in range(1, at.stacks):
        first_stack_copy(s).wait()
    value = f_stack[0]
    for s in range(1, at.stacks):
        value = value + f_stack[s]
    g_first[...] = value * (1.0 / (side * mx))
    gp_sum.plane_back_wait()

    def grads_copy():
        return remote(gp_all.at[core], gp_all.at[core], core_send.at[4], core_recv.at[4], partner)

    grads_copy().start()
    grads_copy().wait()

    def tile(h, index):
        start, size = spots[index]
        return gp_all[h, start : start + size].reshape(size * 8, LANES) * (1.0 / mx)

    cols = channels // LANES
    for h in range(2):
        for c in range(cols):
            g_second[
                h * (pairs // 2) : (h + 1) * (pairs // 2), c * LANES : (c + 1) * LANES
            ] = tile(h, c)
    low = lax.broadcasted_iota(jnp.int32, (rd, LANES), 1) < half
    for j in range(rb // 2):
        t0, t1 = tile(0, cols + j), tile(1, cols + j)
        g_third[2 * j] = jnp.where(low, t0, pltpu.roll(t1, half, 1))
        g_third[2 * j + 1] = jnp.where(low, pltpu.roll(t0, half, 1), t1)
    for q in range(2):
        g_fourth[q] = tile(0, cols + rb // 2 + q) + tile(1, cols + rb // 2 + q)
    for i in range(steps):
        rows_copy(i).wait()


def output_kernel(table, rows, out):
    chan, n, side = out.shape
    out[...] = dot(rows[...].reshape(chan * n, rows.shape[2]), table[...]).astype(BF16).reshape(
        out.shape
    )


def input_kernel(first, table, rows, out, kron):
    rank, _, wide = rows.shape
    chan, _, side = out.shape

    @pl.when(pl.program_id(0) == 0)
    def _():
        kron[...] = spread(first[...], chan)

    block = dot(kron[...], rows[...].reshape(rank * STEP, wide)) * (1.0 / side)
    out[...] = dot(block.astype(BF16), table[...]).astype(BF16).reshape(out.shape)


def whole(shape):
    return pl.BlockSpec(shape, lambda i: (0,) * len(shape))


def local(input_field, out_cotangent, core_first, core_second, core_third, column_mode_core):
    grid_count, chan_count = lax.axis_size("grid"), lax.axis_size("chan")
    grid_index = lax.axis_index("grid")
    chan_index = lax.axis_index("chan")
    chan, rows, side = input_field.shape
    channels, rank_a = core_first.shape
    rank_b, modes_x, rank_d = core_third.shape
    modes_y = column_mode_core.shape[2]
    wide = 2 * modes_y
    half = modes_x // 2
    both = 2 * chan
    pairs = rank_a * rank_b

    table_np = width_table(side, modes_y)
    table = jnp.asarray(table_np)
    table_t = jnp.asarray(np.ascontiguousarray(table_np.T))
    turns = turn_table(side, modes_x).reshape(2, modes_x, grid_count, rows)
    turns = jnp.asarray(np.ascontiguousarray(turns.transpose(2, 0, 1, 3)))
    cs = lax.dynamic_index_in_dim(turns, grid_index, 0, keepdims=False)

    first_local = lax.dynamic_slice_in_dim(core_first, chan_index * chan, chan, 0).astype(BF16)
    second = core_second.transpose(0, 2, 1).reshape(pairs, channels)
    second = lax.dynamic_slice_in_dim(second, chan_index // 2 * both, both, 1)
    third = lax.dynamic_slice_in_dim(
        core_third.transpose(0, 2, 1), chan_index % 2 * half, half, 2
    )

    row_steps = rows // STEP
    row_modes, lead, csf, csb = pl.pallas_call(
        lead_kernel,
        grid=(row_steps,),
        in_specs=[
            whole((rank_a, chan)),
            whole((side, wide)),
            whole((2, modes_x, rows)),
            pl.BlockSpec((chan, STEP, side), lambda i: (0, i, 0)),
        ],
        out_specs=[
            pl.BlockSpec((chan, STEP, wide), lambda i: (0, i, 0)),
            whole((modes_x, 2, rank_a, modes_y)),
            whole((2 * modes_x, 2 * rows)),
            whole((2 * rows, 2 * modes_x)),
        ],
        out_shape=[
            jax.ShapeDtypeStruct((chan, rows, wide), BF16),
            jax.ShapeDtypeStruct((modes_x, 2, rank_a, modes_y), BF16),
            jax.ShapeDtypeStruct((2 * modes_x, 2 * rows), BF16),
            jax.ShapeDtypeStruct((2 * rows, 2 * modes_x), BF16),
        ],
        scratch_shapes=[
            pltpu.VMEM((rank_a * STEP, chan * STEP), BF16),
            pltpu.VMEM((rank_a // 2, 2 * rows, wide), BF16),
            pltpu.VMEM((rank_a, 2 * modes_x, modes_y), F32),
        ],
        compiler_params=params(),
        name="lead",
    )(first_local.T, table, cs, input_field)

    planes, stacks = chan_count, grid_count // 2
    tiles = 2 * half
    owners = planes * stacks
    grad_tiles = (pairs // 2 * channels + rank_d * rank_b * half + rank_d * wide) // (8 * LANES)
    grad_tiles += -grad_tiles % owners
    sub = min(8, STEP)
    subs = chan // sub
    slots = min(4, subs)
    blocks = chan // STEP
    groups = half // STEP
    peers = max(planes, stacks) - 1
    steps = chan // 8

    def reduce_buffers(count, shape, dtype):
        chunk = count // planes
        return [
            pltpu.VMEM((planes - 1, chunk, *shape), dtype),
            pltpu.VMEM((stacks - 1, chunk // stacks, *shape), dtype),
            pltpu.VMEM((chunk, *shape), dtype),
        ]

    tile = (rank_a, modes_y)
    scratch = [
        pltpu.VMEM((slots, sub, rows, side), BF16),
        pltpu.VMEM((chan, rows, wide), BF16),
        pltpu.VMEM((chan, rows, wide), BF16),
        pltpu.VMEM((sub // 2, 2 * rows, wide), BF16),
        pltpu.VMEM((STEP, 2 * modes_x, modes_y), F32),
        pltpu.VMEM((blocks, modes_x, STEP, wide), BF16),
        pltpu.VMEM((half, both, wide), BF16),
        pltpu.VMEM((groups, chan, 2, STEP, wide), BF16),
        pltpu.VMEM((chan // 2, 2, modes_x, wide), BF16),
        pltpu.VMEM((pairs, both), BF16),
        pltpu.VMEM((pairs, both), BF16),
        pltpu.VMEM((both, pairs), BF16),
        pltpu.VMEM((half, rank_b, wide), F32),
        pltpu.VMEM((half, rank_a, wide), F32),
        pltpu.VMEM((half * rank_b, wide), F32),
        pltpu.VMEM((pairs, 2 * wide), BF16),
        pltpu.VMEM((STEP, both, wide), F32),
        pltpu.VMEM((pairs, both), F32),
        pltpu.VMEM((rank_a // 2, 2 * modes_x, wide), BF16),
        pltpu.VMEM((chan * STEP, rank_a * STEP), F32),
        pltpu.VMEM((half, 2, *tile), BF16),
        pltpu.VMEM((tiles, *tile), BF16),
        pltpu.VMEM((tiles, *tile), BF16),
        *reduce_buffers(tiles, tile, BF16),
        pltpu.VMEM((tiles, *tile), BF16),
        pltpu.VMEM((2, tiles, *tile), BF16),
        *reduce_buffers(tiles, tile, BF16),
        pltpu.VMEM((pairs // 2, both), F32),
        pltpu.VMEM((grad_tiles, 8, LANES), F32),
        pltpu.VMEM((2, grad_tiles, 8, LANES), F32),
        *reduce_buffers(grad_tiles, (8, LANES), F32),
        pltpu.VMEM((2, rank_a, channels), F32),
        pltpu.VMEM((planes, rank_a, channels), F32),
        pltpu.VMEM((stacks, rank_a, channels), F32),
        *[pltpu.SemaphoreType.DMA((4, peers))] * 6,
        *[pltpu.SemaphoreType.DMA((5,))] * 2,
        *[pltpu.SemaphoreType.DMA((blocks,))] * 2,
        *[pltpu.SemaphoreType.DMA((groups,))] * 2,
        *[pltpu.SemaphoreType.DMA((2, peers))] * 2,
        pltpu.SemaphoreType.DMA((slots,)),
        pltpu.SemaphoreType.DMA,
        pltpu.SemaphoreType.DMA((steps,)),
    ]
    vmem = pl.BlockSpec(memory_space=pltpu.VMEM)
    anywhere = pl.BlockSpec(memory_space=pl.ANY)
    out_rows, back_rows, g_first, g_second, g_third, g_fourth = pl.pallas_call(
        spectral_kernel,
        in_specs=[anywhere, anywhere] + [vmem] * 7,
        out_specs=[anywhere] + [vmem] * 5,
        out_shape=[
            jax.ShapeDtypeStruct((chan, rows, wide), BF16),
            jax.ShapeDtypeStruct((rank_a, rows, wide), BF16),
            jax.ShapeDtypeStruct((rank_a, channels), F32),
            jax.ShapeDtypeStruct((pairs, channels), F32),
            jax.ShapeDtypeStruct((rank_b, rank_d, modes_x), F32),
            jax.ShapeDtypeStruct((2, rank_d, modes_y), F32),
        ],
        scratch_shapes=scratch,
        compiler_params=pltpu.CompilerParams(
            collective_id=0, has_side_effects=True, vmem_limit_bytes=62 * 2**20
        ),
        name="spectral",
    )(out_cotangent, row_modes, lead, csf, csb, table, second, third, column_mode_core)

    out_step = min(chan, 8)
    output_field = pl.pallas_call(
        output_kernel,
        grid=(chan // out_step,),
        in_specs=[
            whole((wide, side)),
            pl.BlockSpec((out_step, rows, wide), lambda i: (i, 0, 0)),
        ],
        out_specs=pl.BlockSpec((out_step, rows, side), lambda i: (i, 0, 0)),
        out_shape=jax.ShapeDtypeStruct((chan, rows, side), BF16),
        compiler_params=params(),
        name="output",
    )(table_t, out_rows)

    input_grad = pl.pallas_call(
        input_kernel,
        grid=(row_steps,),
        in_specs=[
            whole((chan, rank_a)),
            whole((wide, side)),
            pl.BlockSpec((rank_a, STEP, wide), lambda i: (0, i, 0)),
        ],
        out_specs=pl.BlockSpec((chan, STEP, side), lambda i: (0, i, 0)),
        out_shape=jax.ShapeDtypeStruct((chan, rows, side), BF16),
        scratch_shapes=[pltpu.VMEM((chan * STEP, rank_a * STEP), BF16)],
        compiler_params=params(),
        name="input_grad",
    )(first_local, table_t, back_rows)

    return (
        output_field,
        input_grad,
        g_first.T,
        g_second.reshape(rank_a, rank_b, channels).transpose(0, 2, 1),
        g_third.transpose(0, 2, 1),
        g_fourth,
    )


def solution(mesh):
    placed = (P("chan", "grid", None), P("chan", "grid", None), P(), P(), P(), P())
    return jax.shard_map(
        local,
        mesh=mesh,
        in_specs=placed,
        out_specs=(P("chan", "grid", None), P("chan", "grid", None), P(), P(), P(), P()),
        check_vma=False,
    )
```

time: 239 us -> 132 us (0.55)
  Pallas kernels: 214 us -> 116 us
  local copies, waits for them, and re-layouts: 21.6 us -> 15.2 us
    pallas_call x7 -> x2, Pallas kernels: 189 us -> 92.6 us  [the longest x1 83.7 us: local(): pl.pallas_call(spectral_kernel, in_specs=[anywhere, anywhere] + [vmem] *...]
    reshape x8 -> x0, local copies, waits for them, and re-layouts: 5.93 us -> none  [the longest x1 2.18 us: local(): grad_third = three.reshape(mode_steps, rank_d, STEP, rank_b).transpose(3,...]
    transpose x6 -> x1, local copies, waits for them, and re-layouts: 4.03 us -> 0.07 us  [local(): row_modes, lead, csf, csb = pl.pallas_call(lead_kernel, grid=(row_steps,)...]
    unnamed x20 -> x33, local copies, waits for them, and re-layouts: 8.86 us -> 11.2 us
where the time goes in v1:
time: 132 us; the launch traced here: 131 us
  Pallas kernels  116 us (88%)
  local copies, waits for them, and re-layouts  15.2 us (12%)
    pallas_call x1, Pallas kernels, local(): pl.pallas_call(spectral_kernel, in_specs=[anywhere, anywhere] + [vmem] *...  83.7 us
    pallas_call x1, Pallas kernels, local(): pl.pallas_call(lead_kernel, grid=(row_steps,), in_specs=[whole((rank_a, c...  13.2 us
    unnamed x33, local copies, waits for them, and re-layouts  11.2 us
    pallas_call x1, Pallas kernels, local(): pl.pallas_call(input_kernel, grid=(row_steps,), in_specs=[whole((chan, ra...  9.82 us
    pallas_call x1, Pallas kernels, local(): pl.pallas_call(output_kernel, grid=(chan // out_step,), in_specs=[whole((...  8.86 us

profile of v1, /device:TPU:0, one launch (start us, length us, event | category | flops | bytes accessed | tf_op | source)
XLA Modules:
  0.0 131.5 jit_solution(9461378755542934739)
XLA Ops:
  0.6 0.0 copy-start
  0.7 0.9 copy-done
  1.6 0.8 constant_dynamic-slice_fusion.1
  2.4 0.1 copy.17.first
  2.5 0.1 copy.16.first_t
  2.5 0.9 dynamic-slice_bitcast_fusion.1.cs
  3.4 0.7 constant_dynamic-slice_fusion.second
  4.1 1.7 %dynamic-slice_bitcast_fusion.third = f32[16,16,64]{2,1,0:T(8,128)} fusion(f32[16,128,16]{1,2,0:T(8,128)} %param.13, s32[]{:T(128)S(6)} %select_n.29), kind=kLoop, calls=%fused_computation | loop fusion | bytes 131076 | tf_op jit(solution)/shard_map/dynamic_slice | solution.py:667
  5.7 1.0 copy-done.4
  6.8 13.2 %lead.1 = (bf16[64,128,256]{2,1,0:T(8,128)(2,1)S(1)}, bf16[128,2,16,128]{3,2,1,0:T(8,128)(2,1)S(1)}, bf16[256,256]{1,0:T(8,128)(2,1)S(1)}, bf16[256,256]{1,0:T(8,128)(2,1)S(1)}) custom-call(bf16[16,64]{1,0:T(8,128)(2,1)S(1)} %copy.16.first_t, bf16[1024,256]{1,0:T(8,128)(2,1)S(1)} %copy-done.4, bf16[2,128,128]{2,1,0:T(8,128)(2,1)S(1)} %dynamic-slice_bitcast_fusion.1.cs, ...), custom_call_target="tpu_custom_call" | custom-call | tf_op jit(solution)/shard_map/lead/pallas_call | solution.py:672
  19.9 0.0 copy-start.2
  19.9 2.0 %copy-done.2 = bf16[64,128,256]{2,1,0:T(8,128)(2,1)} copy-done((bf16[64,128,256]{2,1,0:T(8,128)(2,1)}, bf16[64,128,256]{2,1,0:T(8,128)(2,1)S(1)}, u32[]{:S(2)}) %copy-start.2) | copy-done | bytes 4194328
  21.9 1.0 copy-done.6
  22.9 0.7 copy-done.8
  23.6 0.7 copy-done.9
  24.2 83.7 %spectral.1 = (bf16[64,128,256]{2,1,0:T(8,128)(2,1)}, bf16[16,128,256]{2,1,0:T(8,128)(2,1)}, f32[16,256]{1,0:T(8,128)}, f32[256,256]{1,0:T(8,128)}, f32[16,16,128]{2,1,0:T(8,128)}, /*index=5*/f32[2,16,128]{2,1,0:T(8,128)}) custom-call(bf16[64,128,1024]{2,1,0:T(8,128)(2,1)} %cot.1, bf16[64,128,256]{2,1,0:T(8,128)(2,1)} %copy-done.2, ...), custom_call_target="tpu_custom_call" | custom-call | tf_op jit(solution)/shard_map/spectral/pallas_call | solution.py:770
  108.0 0.0 copy-start.1
  108.0 2.2 %copy-done.3 = bf16[64,128,256]{2,1,0:T(8,128)(2,1)S(1)} copy-done((bf16[64,128,256]{2,1,0:T(8,128)(2,1)S(1)}, bf16[64,128,256]{2,1,0:T(8,128)(2,1)}, u32[]{:S(2)}) %copy-start.3) | copy-done | bytes 4194328
  110.2 8.9 %output.1 = bf16[64,128,1024]{2,1,0:T(8,128)(2,1)} custom-call(bf16[256,1024]{1,0:T(8,128)(2,1)S(1)} %copy-done.5, bf16[64,128,256]{2,1,0:T(8,128)(2,1)S(1)} %copy-done.3), custom_call_target="tpu_custom_call" | custom-call | tf_op jit(solution)/shard_map/output/pallas_call | solution.py:790
  119.1 9.8 %input_grad.1 = bf16[64,128,1024]{2,1,0:T(8,128)(2,1)} custom-call(bf16[64,16]{1,0:T(8,128)(2,1)S(1)} %copy.17.first, bf16[256,1024]{1,0:T(8,128)(2,1)S(1)} %copy-done.5, bf16[16,128,256]{2,1,0:T(8,128)(2,1)S(1)} %copy-done.7), custom_call_target="tpu_custom_call" | custom-call | tf_op jit(solution)/shard_map/input_grad/pallas_call | solution.py:803
  128.9 0.6 copy.22
  129.5 0.7 copy.23
  130.2 0.7 copy.24
  130.9 0.6 copy.25
  (18 shorter events, 0.0 us)
Async XLA Ops:
  0.6 1.0 copy-start
  5.7 1.0 copy-start.4
  6.8 101.2 %copy-start.5 = (bf16[256,1024]{1,0:T(8,128)(2,1)S(1)}, bf16[256,1024]{1,0:T(8,128)(2,1)}, u32[]{:S(2)}) copy-start(bf16[256,1024]{1,0:T(8,128)(2,1)} %constant.52.clone.table) | copy-start | bytes 1572868
  19.9 2.0 %copy-start.2 = (bf16[64,128,256]{2,1,0:T(8,128)(2,1)}, bf16[64,128,256]{2,1,0:T(8,128)(2,1)S(1)}, u32[]{:S(2)}) copy-start(bf16[64,128,256]{2,1,0:T(8,128)(2,1)S(1)} %get-tuple-element.16.modes_in) | copy-start | bytes 12582916
  21.9 1.0 copy-start.6
  22.9 0.7 copy-start.8
  23.6 0.7 copy-start.9
  108.0 23.5 %copy-start.1 = (f32[16,256,16]{1,2,0:T(8,128)S(1)}, f32[16,256,16]{1,2,0:T(8,128)}, u32[]{:S(2)}) copy-start(f32[16,256,16]{1,2,0:T(8,128)} %param.12) | copy-start | bytes 786436
  108.0 2.2 %copy-start.3 = (bf16[64,128,256]{2,1,0:T(8,128)(2,1)S(1)}, bf16[64,128,256]{2,1,0:T(8,128)(2,1)}, u32[]{:S(2)}) copy-start(bf16[64,128,256]{2,1,0:T(8,128)(2,1)} %get-tuple-element.20.rows) | copy-start | bytes 12582916
  110.2 8.9 %copy-start.7 = (bf16[16,128,256]{2,1,0:T(8,128)(2,1)S(1)}, bf16[16,128,256]{2,1,0:T(8,128)(2,1)}, u32[]{:S(2)}) copy-start(bf16[16,128,256]{2,1,0:T(8,128)(2,1)} %get-tuple-element.21.rows) | copy-start | bytes 3145732
  110.2 18.7 %copy-start.13 = (f32[16,256]{1,0:T(8,128)S(1)}, f32[16,256]{1,0:T(8,128)}, u32[]{:S(2)}) copy-start(f32[16,256]{1,0:T(8,128)} %get-tuple-element.22) | copy-start | bytes 49156
  110.2 19.3 %copy-start.10 = (f32[256,256]{1,0:T(8,128)S(1)}, f32[256,256]{1,0:T(8,128)}, u32[]{:S(2)}) copy-start(f32[256,256]{1,0:T(8,128)} %get-tuple-element.23) | copy-start | bytes 786436
  110.2 20.0 %copy-start.11 = (f32[16,16,128]{2,1,0:T(8,128)S(1)}, f32[16,16,128]{2,1,0:T(8,128)}, u32[]{:S(2)}) copy-start(f32[16,16,128]{2,1,0:T(8,128)} %get-tuple-element.24) | copy-start | bytes 393220
  110.2 20.7 %copy-start.12 = (f32[2,16,128]{2,1,0:T(8,128)S(1)}, f32[2,16,128]{2,1,0:T(8,128)}, u32[]{:S(2)}) copy-start(f32[2,16,128]{2,1,0:T(8,128)} %get-tuple-element.37) | copy-start | bytes 49156

commit v2 on v1

v2 whole, which is shorter than its diff:
```python
import math

import jax
import jax.numpy as jnp
import numpy as np
from jax import lax
from jax.experimental import pallas as pl
from jax.experimental.pallas import tpu as pltpu
from jax.sharding import PartitionSpec as P

F32 = jnp.float32
BF16 = jnp.bfloat16
HI = lax.Precision.HIGHEST
STEP = 16
LANES = 128
SLOTS = 3
MESH = pl.DeviceIdType.MESH


def params(mib=48):
    return pltpu.CompilerParams(vmem_limit_bytes=mib * 2**20)


def dot(a, b, precision=None):
    return jnp.dot(a, b, preferred_element_type=F32, precision=precision)


def dot_nt(a, b, precision=None):
    return lax.dot_general(
        a, b, (((1,), (1,)), ((), ())), preferred_element_type=F32, precision=precision
    )


def dot_tn(a, b, precision=None):
    return lax.dot_general(
        a, b, (((0,), (0,)), ((), ())), preferred_element_type=F32, precision=precision
    )


def width_table(side, modes_y):
    phase = np.arange(side)[:, None] * np.arange(modes_y)[None, :] % side
    angle = phase.astype(np.float32) * np.float32(2.0 * math.pi / side)
    return np.concatenate([np.cos(angle), -np.sin(angle)], axis=1).astype(BF16)


def turn_table(side, modes_x):
    kx = np.arange(modes_x)
    freq = np.where(kx < modes_x // 2, kx, side - modes_x + kx)
    phase = freq[:, None] * np.arange(side)[None, :] % side
    angle = phase.astype(np.float32) * np.float32(2.0 * math.pi / side)
    return np.stack([np.cos(angle), np.sin(angle)]).astype(BF16)


def one_hot(rows, cols, offset):
    row = lax.broadcasted_iota(jnp.int32, (rows, cols), 0)
    col = lax.broadcasted_iota(jnp.int32, (rows, cols), 1)
    return col == row + offset


def spread(values, rows, n, offset=0):
    lane = lax.broadcasted_iota(jnp.int32, (values.shape[1], n * STEP), 1)
    row = lax.broadcasted_iota(jnp.int32, (values.shape[1], n * STEP), 0)
    wide = dot(values, (lane // STEP + offset == row).astype(BF16))
    at = lax.broadcasted_iota(jnp.int32, (STEP, n * STEP), 1) % STEP
    unit = (at == lax.broadcasted_iota(jnp.int32, (STEP, n * STEP), 0)).astype(F32)
    return (wide[:, None, :] * unit[None]).reshape(rows * STEP, n * STEP).astype(BF16)


def flip(index, bits):
    bit = 1
    while bit <= bits:
        if bits & bit:
            index = index + bit * (1 - 2 * (index // bit % 2))
        bit *= 2
    return index


class Place:
    def __init__(self):
        self.grid, self.chan = lax.axis_index("grid"), lax.axis_index("chan")
        self.core = self.chan % 2
        self.planes = lax.axis_size("chan")
        self.stacks = lax.axis_size("grid") // 2
        self.plane = self.chan // 2 * 2 + self.grid % 2
        self.stack = self.grid // 2

    def across_core(self):
        return {"grid": self.grid, "chan": flip(self.chan, 1)}

    def across_plane(self, s):
        return {"grid": flip(self.grid, s % 2), "chan": flip(self.chan, s // 2 * 2)}

    def across_stack(self, s):
        return {"grid": flip(self.grid, s * 2), "chan": self.chan}

    def peers(self):
        return (
            [self.across_core()]
            + [self.across_plane(s) for s in range(1, self.planes)]
            + [self.across_stack(s) for s in range(1, self.stacks)]
        )


def remote(src, dst, send, recv, peer):
    return pltpu.make_async_remote_copy(
        src_ref=src, dst_ref=dst, send_sem=send, recv_sem=recv,
        device_id=peer, device_id_type=MESH,
    )


class Reduce:
    def __init__(self, place, source, result, land_plane, land_stack, mid, send, recv):
        self.at, self.source, self.result = place, source, result
        self.land_plane, self.land_stack, self.mid = land_plane, land_stack, mid
        self.send, self.recv = send, recv
        self.chunk = source.shape[0] // place.planes
        self.piece = self.chunk // place.stacks

    def plane_copy(self, s):
        there = flip(self.at.plane, s)
        return remote(
            self.source.at[pl.ds(there * self.chunk, self.chunk)],
            self.land_plane.at[s - 1],
            self.send.at[0, s - 1], self.recv.at[0, s - 1], self.at.across_plane(s),
        )

    def plane_send(self):
        for s in range(1, self.at.planes):
            self.plane_copy(s).start()

    def plane_wait(self):
        for s in range(1, self.at.planes):
            self.plane_copy(s).wait()
        total = self.source[pl.ds(self.at.plane * self.chunk, self.chunk)].astype(F32)
        for s in range(1, self.at.planes):
            total = total + self.land_plane[s - 1].astype(F32)
        self.mid[...] = total.astype(self.mid.dtype)

    def stack_copy(self, s):
        there = flip(self.at.stack, s)
        return remote(
            self.mid.at[pl.ds(there * self.piece, self.piece)],
            self.land_stack.at[s - 1],
            self.send.at[1, s - 1], self.recv.at[1, s - 1], self.at.across_stack(s),
        )

    def stack_send(self):
        for s in range(1, self.at.stacks):
            self.stack_copy(s).start()

    def own(self):
        return pl.ds(self.at.plane * self.chunk + self.at.stack * self.piece, self.piece)

    def stack_wait(self):
        for s in range(1, self.at.stacks):
            self.stack_copy(s).wait()
        total = self.mid[pl.ds(self.at.stack * self.piece, self.piece)].astype(F32)
        for s in range(1, self.at.stacks):
            total = total + self.land_stack[s - 1].astype(F32)
        self.result[self.own()] = total.astype(self.result.dtype)

    def stack_back_copy(self, s):
        return remote(
            self.result.at[self.own()], self.result.at[self.own()],
            self.send.at[2, s - 1], self.recv.at[2, s - 1], self.at.across_stack(s),
        )

    def stack_back_send(self):
        for s in range(1, self.at.stacks):
            self.stack_back_copy(s).start()

    def stack_back_wait(self):
        for s in range(1, self.at.stacks):
            self.stack_back_copy(s).wait()

    def plane_back_copy(self, s):
        here = pl.ds(self.at.plane * self.chunk, self.chunk)
        return remote(
            self.result.at[here], self.result.at[here],
            self.send.at[3, s - 1], self.recv.at[3, s - 1], self.at.across_plane(s),
        )

    def plane_back_send(self):
        for s in range(1, self.at.planes):
            self.plane_back_copy(s).start()

    def plane_back_wait(self):
        for s in range(1, self.at.planes):
            self.plane_back_copy(s).wait()


def spectral_kernel(
    field, cot, turns_in, table, first_t, second, third, column,
    rows_out, back_rows, g_first, g_second, g_third, g_fourth,
    block_v, modes_v, y, held, spec_stage, spec, s_stage, spec_out, cs, csf, csb, kron, mixed,
    by_ab, by_ba, by_t, kern, lead_f, kgrad, outer, held_o, part_second, back_in, total,
    lead_v, lead_core, lead_x, lead_res, lead_lp, lead_ls, lead_mid,
    lg_x, lg_all, lg_lp, lg_ls, lg_mid,
    gp_core, gp_x, gp_all, gp_lp, gp_ls, gp_mid,
    f_core, f_plane, f_stack,
    lead_send, lead_recv, lg_send, lg_recv, gp_send, gp_recv,
    core_send, core_recv, spec_send, spec_recv, out_send, out_recv, f_send, f_recv,
    block_sem, turns_sem, rows_sem,
):
    if outer.shape[0] * outer.shape[1] * 2 < kern.shape[0]:
        outer = block_v
    at = Place()
    core = at.core
    other = 1 - core
    chan, n, side = cot.shape
    wide = table.shape[1]
    my = wide // 2
    mx = cs.shape[1]
    half = mx // 2
    ra, rb, rd = first_t.shape[0], third.shape[0], third.shape[1]
    pairs = ra * rb
    both = 2 * chan
    channels = g_first.shape[1]
    slots, sub = block_v.shape[:2]
    subs = chan // sub
    parts = lead_lp.shape[0]
    row_groups = n // STEP
    lane = lax.broadcasted_iota(jnp.int32, (1, wide), 1)
    weight = jnp.where(lane % my == 0, 1.0, 2.0) * (1.0 / side)
    partner = at.across_core()

    def block_copy(source, j, k):
        slot = lax.rem(k, slots)
        return pltpu.make_async_copy(
            source.at[pl.ds(j * sub, sub)], block_v.at[slot], block_sem.at[slot]
        )

    def fetch(k):
        @pl.when(k < subs)
        def _():
            block_copy(field, k, k).start()

        @pl.when(jnp.logical_and(k >= subs, k < 2 * subs))
        def _():
            block_copy(cot, k - subs, k).start()

    def rows_of_block(source, j, k):
        block_copy(source, j, k).wait()
        block = block_v[lax.rem(k, slots)].reshape(sub * n, side)
        product = dot(block, table[...]).astype(BF16)
        fetch(k + slots)
        return product

    barrier = pltpu.get_barrier_semaphore()
    peers = at.peers()
    for peer in peers:
        pl.semaphore_signal(barrier, inc=1, device_id=peer, device_id_type=MESH)
    for k in range(min(slots, 2 * subs)):
        fetch(jnp.int32(k))
    turns_copy = pltpu.make_async_copy(turns_in.at[at.grid], cs, turns_sem)
    turns_copy.start()
    kron[...] = spread(first_t[...].astype(BF16), ra, chan, at.chan * chan)
    turns_copy.wait()
    c, s = cs[0], cs[1]
    csf[:mx, :n], csf[:mx, n:], csf[mx:, :n], csf[mx:, n:] = c, s, -s, c
    ct = jnp.swapaxes(c.astype(F32), 0, 1).astype(BF16)
    st = jnp.swapaxes(s.astype(F32), 0, 1).astype(BF16)
    csb[:n, :mx], csb[:n, mx:], csb[n:, :mx], csb[n:, mx:] = ct, -st, st, ct

    mixed[...] = jnp.zeros_like(mixed)

    def field_body(i, carry):
        product = rows_of_block(field, i, i)
        shaped = product.reshape(sub, n, wide)
        modes_v[pl.ds(i * sub, sub)] = shaped
        for g in range(row_groups):
            y[: sub * STEP, g * wide : (g + 1) * wide] = shaped[
                :, g * STEP : (g + 1) * STEP
            ].reshape(sub * STEP, wide)
        part = pl.ds(pl.multiple_of(i * sub * STEP, sub * STEP), sub * STEP)
        mixed[...] += dot(kron[:, part], y[: sub * STEP, : row_groups * wide])
        return carry

    lax.fori_loop(0, subs, field_body, 0)
    for g in range(row_groups):
        for q in range(2):
            for a in range(ra):
                back_in[q * n + g * STEP : q * n + (g + 1) * STEP, a * my : (a + 1) * my] = mixed[
                    a * STEP : (a + 1) * STEP, g * wide + q * my : g * wide + (q + 1) * my
                ].astype(BF16)
    z = dot(csf[...], back_in[: 2 * n]) * (1.0 / side)
    for a in range(ra):
        held[a] = z[:, a * my : (a + 1) * my]
    turned = jnp.swapaxes(held[...], 0, 1).astype(BF16)
    lead_v[:, 0] = turned[:mx]
    lead_v[:, 1] = turned[mx:]

    def lead_core_copy():
        return remote(
            lead_v.at[pl.ds(other * half, half)], lead_core,
            core_send.at[0], core_recv.at[0], partner,
        )

    pl.semaphore_wait(barrier, len(peers))
    lead_core_copy().start()

    if second.shape[1] > both and both % LANES == 0:
        sec = second[:, pl.ds(pl.multiple_of(at.chan // 2 * both, both), both)]
    else:
        sec = second[...]
    by_ab[...] = sec.astype(BF16)
    by_ba[...] = jnp.swapaxes(sec.reshape(ra, rb, both), 0, 1).reshape(pairs, both).astype(BF16)
    by_t[...] = jnp.swapaxes(sec, 0, 1).astype(BF16)
    col = jnp.concatenate([column[0], column[1]], axis=1)
    for b in range(rb):
        held_o[b, :mx] = dot_tn(third[b], col, HI)
    own_half = pl.ds(pl.multiple_of(core * half, half), half)
    kern[...] = jnp.swapaxes(held_o[:, own_half, :], 0, 1)

    def sums(source, result, land_plane, land_stack, mid, send, recv):
        share = source.shape[0] // parts
        made = []
        for p in range(parts):
            where = pl.ds(p * share, share)
            made.append(Reduce(
                at, source.at[where], result(where), land_plane.at[p], land_stack.at[p],
                mid.at[p], send.at[p], recv.at[p],
            ))
        return made

    lead_sums = sums(
        lead_x, lambda w: lead_res.at[w], lead_lp, lead_ls, lead_mid, lead_send, lead_recv
    )
    lg_sums = sums(
        lg_x, lambda w: lg_all.at[core, w], lg_lp, lg_ls, lg_mid, lg_send, lg_recv
    )
    gp_sum = Reduce(at, gp_x, gp_all.at[core], gp_lp, gp_ls, gp_mid, gp_send, gp_recv)

    lead_core_copy().wait()
    mine = lead_v[pl.ds(core * half, half)].astype(F32) + lead_core[...].astype(F32)
    lead_x[...] = mine.reshape(lead_x.shape).astype(BF16)
    for r in lead_sums:
        r.plane_send()

    def plan(hooks, index):
        for when, todo in hooks:
            @pl.when(index == when)
            def _():
                for step in todo:
                    step()

    def spec_copy(i):
        return remote(
            spec_stage.at[i, pl.ds(other * half, half)],
            spec.at[:, pl.ds(core * chan + i * STEP, STEP), :],
            spec_send.at[i], spec_recv.at[i], partner,
        )

    first_lead, last_lead = lead_sums[0], lead_sums[-1]
    first_lg, last_lg = lg_sums[0], lg_sums[-1]
    split = parts > 1

    def both_of(one, two):
        return [one] + ([two] if split else [])

    cot_hooks = [
        (min(1, subs - 1), [first_lead.plane_wait, first_lead.stack_send]),
        (min(2, subs - 1), [last_lead.plane_wait, last_lead.stack_send] if split else []),
        (min(3, subs - 1), [first_lead.stack_wait, first_lead.stack_back_send]),
    ]

    def cot_body(i, carry):
        product = rows_of_block(cot, i, i + subs)
        for c in range(sub):
            for q in range(2):
                y[q * n : (q + 1) * n, c * my : (c + 1) * my] = product[
                    c * n : (c + 1) * n, q * my : (q + 1) * my
                ]
        z = dot(csf[...], y[: 2 * n, : sub * my])
        for c in range(sub):
            held[c] = z[:, c * my : (c + 1) * my] * weight[:, :my]
        turned = jnp.swapaxes(held[...], 0, 1).astype(BF16)
        spec_stage[i, :, :, :my] = turned[:mx]
        spec_stage[i, :, :, my:] = turned[mx:]
        spec_copy(i).start()
        spec[:, pl.ds(pl.multiple_of(core * chan + i * STEP, STEP), STEP), :] = spec_stage[
            i, pl.ds(core * half, half)
        ]

        plan(cot_hooks, i)
        return carry

    lax.fori_loop(0, subs, cot_body, 0)
    for i in range(subs):
        spec_copy(i).wait()

    unroll = 4

    def back_body(j, carry):
        for u in range(unroll):
            k = j * unroll + u
            g = dot(by_ba[...], spec[k])
            re = jnp.zeros((ra, my), F32)
            im = jnp.zeros((ra, my), F32)
            for b in range(rb):
                gre = g[b * ra : (b + 1) * ra, :my]
                gim = g[b * ra : (b + 1) * ra, my:]
                kre, kim = kern[k, b : b + 1, :my], kern[k, b : b + 1, my:]
                re += gre * kre + gim * kim
                im += gim * kre - gre * kim
            lg_x[2 * k] = re.astype(BF16)
            lg_x[2 * k + 1] = im.astype(BF16)

        plan(back_hooks, j)
        return carry

    rounds = half // unroll
    back_hooks = []
    if split:
        back_hooks = [
            (rounds // 4, [last_lead.stack_wait, last_lead.stack_back_send]),
            (rounds // 2, [first_lg.plane_send]),
            (rounds * 3 // 4, [first_lead.stack_back_wait, first_lead.plane_back_send]),
        ]
    lax.fori_loop(0, rounds, back_body, 0)
    last_lg.plane_send()
    last_lead.stack_back_wait()
    last_lead.plane_back_send()
    part_second[...] = jnp.zeros_like(part_second)

    per = 2
    folded = outer.shape[1] != half // per

    def outer_put(j, a, lanes, value):
        row = a * rb
        if folded:
            lanes += row // (pairs // 2) * per * wide
            row %= pairs // 2
        outer[j // outer.shape[1], j % outer.shape[1], row : row + rb, lanes : lanes + my] = (
            value.astype(BF16)
        )

    def outer_get(j, lanes, size):
        slab = outer.at[j // outer.shape[1], j % outer.shape[1]]
        if not folded:
            return slab[:, lanes : lanes + size]
        low = slab[:, lanes : lanes + size]
        high = slab[:, per * wide + lanes : per * wide + lanes + size]
        return jnp.concatenate([low, high], axis=0)

    def mix_body(j, carry):
        for u in range(per):
            k = j * per + u
            g = dot(by_ab[...], spec[k])
            kr = kern[k]
            kre, kim = kr[:, :my], kr[:, my:]
            re = jnp.zeros((rb, my), F32)
            im = jnp.zeros((rb, my), F32)
            for a in range(ra):
                rows = slice(a * rb, (a + 1) * rb)
                lre, lim = lead_f[k, a : a + 1, :my], lead_f[k, a : a + 1, my:]
                outer_put(j, a, u * wide, kre * lre - kim * lim)
                outer_put(j, a, u * wide + my, kre * lim + kim * lre)
                gre, gim = g[rows, :my], g[rows, my:]
                re += gre * lre + gim * lim
                im += gim * lre - gre * lim
            at_k = pl.ds(pl.multiple_of(k * rb, rb), rb)
            kgrad[at_k, :my] = re
            kgrad[at_k, my:] = im
        rhs = jnp.concatenate([spec[j * per + u] for u in range(per)], axis=1)
        part_second[...] += dot_nt(outer_get(j, 0, per * wide), rhs)

        plan(mix_hooks, j)
        return carry

    turns_of_part = half // per // parts
    if split:
        mix_hooks = [
            (turns_of_part // 4, [first_lg.plane_wait, first_lg.stack_send]),
            (turns_of_part // 2, [last_lg.plane_wait, last_lg.stack_send]),
            (turns_of_part * 3 // 4, [first_lg.stack_wait, first_lg.stack_back_send]),
            (turns_of_part * 9 // 8, [last_lg.stack_wait, last_lg.stack_back_send]),
            (turns_of_part * 5 // 4, [first_lg.stack_back_wait, first_lg.plane_back_send]),
            (turns_of_part * 13 // 8, [last_lg.stack_back_wait, last_lg.plane_back_send]),
        ]
    else:
        mix_hooks = [
            (turns_of_part // 8, [last_lg.plane_wait, last_lg.stack_send]),
            (turns_of_part * 3 // 8, [last_lg.stack_wait, last_lg.stack_back_send]),
            (turns_of_part * 7 // 8, [last_lg.stack_back_wait, last_lg.plane_back_send]),
        ]
    for p in range(parts):
        share = half // parts
        lead_sums[p].plane_back_wait()
        where = pl.ds(p * 2 * share, 2 * share)
        got = lead_res[where].reshape(share, 2, ra, my).astype(F32)
        lead_f[p * share : (p + 1) * share, :, :my] = got[:, 0]
        lead_f[p * share : (p + 1) * share, :, my:] = got[:, 1]
        lax.fori_loop(p * turns_of_part, (p + 1) * turns_of_part, mix_body, 0)

    def second_copy():
        return remote(
            part_second.at[pl.ds(other * (pairs // 2), pairs // 2)], gp_core,
            core_send.at[1], core_recv.at[1], partner,
        )

    def back_copy():
        return remote(lg_all.at[core], lg_all.at[core], core_send.at[2], core_recv.at[2], partner)

    second_copy().start()
    by_mode = jnp.swapaxes(kgrad[...].reshape(half, rb, wide), 0, 1).reshape(rb * half, wide)
    part_third = dot_nt(col, by_mode, HI)
    third_flat = jnp.concatenate(
        [jnp.where(core == 0, third[b][:, :half], third[b][:, half:]) for b in range(rb)], axis=1
    )
    part_fourth = dot(third_flat, by_mode, HI)
    second_copy().wait()
    mine = part_second[pl.ds(core * (pairs // 2), pairs // 2)] + gp_core[...]
    mine = dot(mine, one_hot(both, channels, at.chan // 2 * both).astype(F32), HI)

    pieces = []
    for value in (mine, part_third, part_fourth):
        for c in range(value.shape[1] // LANES):
            pieces.append((value, c))
    spots, count = [], 0
    for value, c in pieces:
        tiles = value.shape[0] // 8
        gp_x[count : count + tiles] = value[:, c * LANES : (c + 1) * LANES].reshape(
            tiles, 8, LANES
        )
        spots.append((count, tiles))
        count += tiles
    if count < gp_x.shape[0]:
        gp_x[count:] = jnp.zeros((gp_x.shape[0] - count, 8, LANES), F32)
    gp_sum.plane_send()
    for r in lg_sums:
        r.plane_back_wait()
    back_copy().start()

    back_copy().wait()
    for q in range(2):
        for h in range(2):
            got = lg_all[h].reshape(half, 2, ra, my)[:, q].astype(F32)
            turned = jnp.swapaxes(got, 0, 1).astype(BF16)
            for a in range(ra):
                back_in[
                    q * mx + h * half : q * mx + (h + 1) * half, a * my : (a + 1) * my
                ] = turned[a]
    r = dot(csb[...], back_in[...]).astype(BF16)
    for a in range(ra):
        for q in range(2):
            back_rows[a, :, q * my : (q + 1) * my] = r[
                q * n : (q + 1) * n, a * my : (a + 1) * my
            ]
    total[...] = jnp.zeros_like(total)

    def first_body(i, carry):
        row = pl.ds(pl.multiple_of(i * STEP, STEP), STEP)
        block = back_rows[:, row, :].reshape(ra * STEP, wide)
        total[...] += dot_nt(modes_v[:, row, :].reshape(chan * STEP, wide), block)
        return carry

    lax.fori_loop(0, n // STEP, first_body, 0)
    shape = (STEP, ra * STEP)
    unit = lax.broadcasted_iota(jnp.int32, shape, 1) % STEP == lax.broadcasted_iota(
        jnp.int32, shape, 0
    )
    kept = total[...].reshape(chan, STEP, ra * STEP) * unit.astype(F32)[None]
    lane_f = lax.broadcasted_iota(jnp.int32, (ra, ra * STEP), 1)
    row_f = lax.broadcasted_iota(jnp.int32, (ra, ra * STEP), 0)
    pick = (lane_f // STEP == row_f).astype(F32)
    part_first = dot_nt(pick, jnp.sum(kept, axis=1), HI)
    f_core[core] = dot(part_first, one_hot(chan, channels, at.chan * chan).astype(F32), HI)

    def first_core_copy():
        return remote(f_core.at[core], f_core.at[core], core_send.at[3], core_recv.at[3], partner)

    def first_plane_copy(s):
        return remote(
            f_plane.at[at.plane], f_plane.at[at.plane],
            f_send.at[0, s - 1], f_recv.at[0, s - 1], at.across_plane(s),
        )

    def first_stack_copy(s):
        return remote(
            f_stack.at[at.stack], f_stack.at[at.stack],
            f_send.at[1, s - 1], f_recv.at[1, s - 1], at.across_stack(s),
        )

    def first_plane():
        first_core_copy().wait()
        f_plane[at.plane] = f_core[0] + f_core[1]
        for s in range(1, at.planes):
            first_plane_copy(s).start()

    def first_stack():
        for s in range(1, at.planes):
            first_plane_copy(s).wait()
        value = f_plane[0]
        for s in range(1, at.planes):
            value = value + f_plane[s]
        f_stack[at.stack] = value
        for s in range(1, at.stacks):
            first_stack_copy(s).start()

    first_core_copy().start()
    gp_sum.plane_wait()
    gp_sum.stack_send()

    def out_copy(g):
        return remote(
            s_stage.at[g, :, :, pl.ds(other * chan * my, chan * my)],
            spec_out.at[:, pl.ds(core * half + g * STEP, STEP), :],
            out_send.at[g], out_recv.at[g], partner,
        )

    def out_body(g, carry):
        for j in range(STEP // per):
            for u in range(per):
                held_o[j * per + u, :both] = dot(
                    by_t[...], outer_get(g * (STEP // per) + j, u * wide, wide)
                )
        turned = jnp.swapaxes(held_o[:, :both], 0, 1).astype(BF16)
        for o in range(both):
            for q in range(2):
                s_stage[g, q, :, o * my : (o + 1) * my] = turned[o, :, q * my : (q + 1) * my]
        out_copy(g).start()
        row = pl.ds(pl.multiple_of(core * half + g * STEP, STEP), STEP)
        lanes = pl.ds(pl.multiple_of(core * chan * my, chan * my), chan * my)
        spec_out[:, row, :] = s_stage[g, :, :, lanes]

        @pl.when(g == 0)
        def _():
            first_plane()

        @pl.when(g == 2)
        def _():
            gp_sum.stack_wait()
            gp_sum.stack_back_send()
            first_stack()

        return carry

    groups = half // STEP
    lax.fori_loop(0, groups, out_body, 0)
    for g in range(groups):
        out_copy(g).wait()

    turns = 8

    def rows_copy(i):
        where = pl.ds(i * turns, turns)
        return pltpu.make_async_copy(modes_v.at[where], rows_out.at[where], rows_sem.at[i])

    def rows_body(i, carry):
        lanes = pl.ds(pl.multiple_of(i * turns * my, turns * my), turns * my)
        r = dot(csb[...], spec_out[:, :, lanes].reshape(2 * mx, turns * my))
        for c in range(turns):
            for q in range(2):
                part = r[q * n : (q + 1) * n, c * my : (c + 1) * my] * weight[:, :my]
                modes_v[i * turns + c, :, q * my : (q + 1) * my] = part.astype(BF16)
        rows_copy(i).start()

        @pl.when(i == 0)
        def _():
            gp_sum.stack_back_wait()
            gp_sum.plane_back_send()

        return carry

    steps = chan // turns
    lax.fori_loop(0, steps, rows_body, 0)
    for s in range(1, at.stacks):
        first_stack_copy(s).wait()
    value = f_stack[0]
    for s in range(1, at.stacks):
        value = value + f_stack[s]
    g_first[...] = value * (1.0 / (side * mx))
    gp_sum.plane_back_wait()

    def grads_copy():
        return remote(gp_all.at[core], gp_all.at[core], core_send.at[4], core_recv.at[4], partner)

    grads_copy().start()
    grads_copy().wait()

    def tile(h, index):
        start, size = spots[index]
        return gp_all[h, start : start + size].reshape(size * 8, LANES) * (1.0 / mx)

    cols = channels // LANES
    for h in range(2):
        for c in range(cols):
            g_second[
                h * (pairs // 2) : (h + 1) * (pairs // 2), c * LANES : (c + 1) * LANES
            ] = tile(h, c)
    low = lax.broadcasted_iota(jnp.int32, (rd, LANES), 1) < half
    for j in range(rb // 2):
        t0, t1 = tile(0, cols + j), tile(1, cols + j)
        g_third[2 * j] = jnp.where(low, t0, pltpu.roll(t1, half, 1))
        g_third[2 * j + 1] = jnp.where(low, pltpu.roll(t0, half, 1), t1)
    for q in range(2):
        g_fourth[q] = tile(0, cols + rb // 2 + q) + tile(1, cols + rb // 2 + q)
    for i in range(steps):
        rows_copy(i).wait()


def output_kernel(
    first_t, table_in, rows_in, back_in, *refs
):
    grads_in, (out, out_back), grads_out = refs[:4], refs[4:6], refs[6:10]
    table, rows, back, out_v, back_v, kron = refs[10:16]
    grads, (in_sem, rows_sem, grad_sem, out_sem, back_sem) = refs[16:20], refs[20:]
    chan, n, side = out.shape
    rank, _, wide = back.shape
    slots, block = out_v.shape[:2]
    steps, row_steps = chan // block, n // STEP
    back_slots = back_v.shape[0]

    def rows_copy(i):
        where = pl.ds(i * block, block)
        return pltpu.make_async_copy(rows_in.at[where], rows.at[where], rows_sem.at[i])

    table_copy = pltpu.make_async_copy(table_in, table, in_sem.at[0])
    back_copy = pltpu.make_async_copy(back_in, back, in_sem.at[1])
    table_copy.start()
    for i in range(steps):
        rows_copy(i).start()
    back_copy.start()
    for i in range(4):
        pltpu.make_async_copy(grads_in[i], grads[i], grad_sem.at[0, i]).start()
    pick = one_hot(chan, first_t.shape[1], lax.axis_index("chan") * chan).astype(BF16)
    first = dot_nt(pick, first_t[...].astype(BF16)).astype(BF16)
    kron[...] = spread(first, chan, rank)

    def out_copy(i):
        slot = lax.rem(i, slots)
        return pltpu.make_async_copy(
            out_v.at[slot], out.at[pl.ds(i * block, block)], out_sem.at[slot]
        )

    def out_body(i, carry):
        rows_copy(i).wait()

        @pl.when(i >= slots)
        def _():
            out_copy(i - slots).wait()

        product = dot(rows[pl.ds(i * block, block)].reshape(block * n, wide), table[...])
        out_v[lax.rem(i, slots)] = product.astype(BF16).reshape(block, n, side)
        out_copy(i).start()
        return carry

    def in_copy(i):
        slot = lax.rem(i, back_slots)
        return pltpu.make_async_copy(
            back_v.at[slot],
            out_back.at[:, pl.ds(pl.multiple_of(i * STEP, STEP), STEP), :],
            back_sem.at[slot],
        )

    def in_body(i, carry):
        @pl.when(i >= back_slots)
        def _():
            in_copy(i - back_slots).wait()

        part = back[:, pl.ds(pl.multiple_of(i * STEP, STEP), STEP), :].reshape(rank * STEP, wide)
        mid = (dot(kron[...], part) * (1.0 / side)).astype(BF16)
        product = dot(mid, table[...])
        back_v[lax.rem(i, back_slots)] = product.astype(BF16).reshape(chan, STEP, side)
        in_copy(i).start()
        return carry

    table_copy.wait()
    lax.fori_loop(0, steps, out_body, 0)
    back_copy.wait()
    for i in range(4):
        pltpu.make_async_copy(grads_in[i], grads[i], grad_sem.at[0, i]).wait()
        pltpu.make_async_copy(grads[i], grads_out[i], grad_sem.at[1, i]).start()
    lax.fori_loop(0, row_steps, in_body, 0)
    for i in range(max(steps - slots, 0), steps):
        out_copy(jnp.int32(i)).wait()
    for i in range(max(row_steps - back_slots, 0), row_steps):
        in_copy(jnp.int32(i)).wait()
    for i in range(4):
        pltpu.make_async_copy(grads[i], grads_out[i], grad_sem.at[1, i]).wait()


def local(input_field, out_cotangent, core_first, core_second, core_third, column_mode_core):
    grid_count, chan_count = lax.axis_size("grid"), lax.axis_size("chan")
    chan_index = lax.axis_index("chan")
    chan, rows, side = input_field.shape
    channels, rank_a = core_first.shape
    rank_b, modes_x, rank_d = core_third.shape
    modes_y = column_mode_core.shape[2]
    wide = 2 * modes_y
    half = modes_x // 2
    both = 2 * chan
    pairs = rank_a * rank_b

    table_np = width_table(side, modes_y)
    table = jnp.asarray(table_np)
    table_t = jnp.asarray(np.ascontiguousarray(table_np.T))
    turns = turn_table(side, modes_x).reshape(2, modes_x, grid_count, rows)
    turns = jnp.asarray(np.ascontiguousarray(turns.transpose(2, 0, 1, 3)))

    first_t = core_first.T
    second = core_second.transpose(0, 2, 1).reshape(pairs, channels)
    if both % LANES:
        second = lax.dynamic_slice_in_dim(second, chan_index // 2 * both, both, 1)
    third = core_third.transpose(0, 2, 1)
    anywhere = pl.BlockSpec(memory_space=pl.ANY)

    row_steps = rows // STEP
    planes, stacks = chan_count, grid_count // 2
    tiles = 2 * half
    owners = planes * stacks
    grad_tiles = (pairs // 2 * channels + rank_d * rank_b * half + rank_d * wide) // (8 * LANES)
    grad_tiles += -grad_tiles % owners
    sub = STEP
    subs = chan // sub
    slots = min(SLOTS, 2 * subs)
    blocks = subs
    fold = rows == pairs // 2 and side == 4 * wide and slots * sub >= half // 2
    outer_shape = (1, 1, 16, LANES) if fold else (1, half // 2, pairs, 2 * wide)
    parts = 2 if tiles % (2 * owners) == 0 else 1
    row_groups = rows // STEP
    wide_y = max(sub * modes_y, row_groups * wide)
    groups = half // STEP
    peers = max(planes, stacks) - 1
    steps = chan // 8

    def reduce_buffers(count, shape, dtype, lead=()):
        chunk = count // planes
        return [
            pltpu.VMEM((*lead, planes - 1, chunk, *shape), dtype),
            pltpu.VMEM((*lead, stacks - 1, chunk // stacks, *shape), dtype),
            pltpu.VMEM((*lead, chunk, *shape), dtype),
        ]

    tile = (rank_a, modes_y)
    scratch = [
        pltpu.VMEM((slots, sub, rows, side), BF16),
        pltpu.VMEM((chan, rows, wide), BF16),
        pltpu.VMEM((max(2 * rows, sub * STEP), wide_y), BF16),
        pltpu.VMEM((STEP, 2 * modes_x, modes_y), F32),
        pltpu.VMEM((blocks, modes_x, STEP, wide), BF16),
        pltpu.VMEM((half, both, wide), BF16),
        pltpu.VMEM((groups, 2, STEP, both * modes_y), BF16),
        pltpu.VMEM((2, modes_x, chan * modes_y), BF16),
        pltpu.VMEM((2, modes_x, rows), BF16),
        pltpu.VMEM((2 * modes_x, 2 * rows), BF16),
        pltpu.VMEM((2 * rows, 2 * modes_x), BF16),
        pltpu.VMEM((rank_a * STEP, chan * STEP), BF16),
        pltpu.VMEM((rank_a * STEP, row_groups * wide), F32),
        pltpu.VMEM((pairs, both), BF16),
        pltpu.VMEM((pairs, both), BF16),
        pltpu.VMEM((both, pairs), BF16),
        pltpu.VMEM((half, rank_b, wide), F32),
        pltpu.VMEM((half, rank_a, wide), F32),
        pltpu.VMEM((half * rank_b, wide), F32),
        pltpu.VMEM(outer_shape, BF16),
        pltpu.VMEM((STEP, max(both, modes_x), wide), F32),
        pltpu.VMEM((pairs, both), F32),
        pltpu.VMEM((2 * modes_x, rank_a * modes_y), BF16),
        pltpu.VMEM((chan * STEP, rank_a * STEP), F32),
        pltpu.VMEM((modes_x, 2, *tile), BF16),
        pltpu.VMEM((half, 2, *tile), BF16),
        pltpu.VMEM((tiles, *tile), BF16),
        pltpu.VMEM((tiles, *tile), BF16),
        *reduce_buffers(tiles // parts, tile, BF16, (parts,)),
        pltpu.VMEM((tiles, *tile), BF16),
        pltpu.VMEM((2, tiles, *tile), BF16),
        *reduce_buffers(tiles // parts, tile, BF16, (parts,)),
        pltpu.VMEM((pairs // 2, both), F32),
        pltpu.VMEM((grad_tiles, 8, LANES), F32),
        pltpu.VMEM((2, grad_tiles, 8, LANES), F32),
        *reduce_buffers(grad_tiles, (8, LANES), F32),
        pltpu.VMEM((2, rank_a, channels), F32),
        pltpu.VMEM((planes, rank_a, channels), F32),
        pltpu.VMEM((stacks, rank_a, channels), F32),
        *[pltpu.SemaphoreType.DMA((parts, 4, peers))] * 4,
        *[pltpu.SemaphoreType.DMA((4, peers))] * 2,
        *[pltpu.SemaphoreType.DMA((5,))] * 2,
        *[pltpu.SemaphoreType.DMA((blocks,))] * 2,
        *[pltpu.SemaphoreType.DMA((groups,))] * 2,
        *[pltpu.SemaphoreType.DMA((2, peers))] * 2,
        pltpu.SemaphoreType.DMA((slots,)),
        pltpu.SemaphoreType.DMA,
        pltpu.SemaphoreType.DMA((steps,)),
    ]
    vmem = pl.BlockSpec(memory_space=pltpu.VMEM)
    out_rows, back_rows, g_first, g_second, g_third, g_fourth = pl.pallas_call(
        spectral_kernel,
        in_specs=[anywhere] * 3 + [vmem] * 5,
        out_specs=[anywhere] + [vmem] * 5,
        out_shape=[
            jax.ShapeDtypeStruct((chan, rows, wide), BF16),
            jax.ShapeDtypeStruct((rank_a, rows, wide), BF16),
            jax.ShapeDtypeStruct((rank_a, channels), F32),
            jax.ShapeDtypeStruct((pairs, channels), F32),
            jax.ShapeDtypeStruct((rank_b, rank_d, modes_x), F32),
            jax.ShapeDtypeStruct((2, rank_d, modes_y), F32),
        ],
        scratch_shapes=scratch,
        compiler_params=pltpu.CompilerParams(
            collective_id=0, has_side_effects=True, vmem_limit_bytes=63 * 2**20
        ),
        name="spectral",
    )(input_field, out_cotangent, turns, table, first_t, second, third, column_mode_core)

    out_step = min(chan, 8)
    out_steps = chan // out_step
    out_slots, back_slots = min(4, out_steps), min(4, row_steps)
    grads = [
        (rank_a, channels), (pairs, channels), (rank_b, rank_d, modes_x), (2, rank_d, modes_y)
    ]
    output_field, input_grad, g_first, g_second, g_third, g_fourth = pl.pallas_call(
        output_kernel,
        in_specs=[vmem] + [anywhere] * 7,
        out_specs=[anywhere] * 6,
        out_shape=[
            jax.ShapeDtypeStruct((chan, rows, side), BF16),
            jax.ShapeDtypeStruct((chan, rows, side), BF16),
            *[jax.ShapeDtypeStruct(shape, F32) for shape in grads],
        ],
        scratch_shapes=[
            pltpu.VMEM((wide, side), BF16),
            pltpu.VMEM((chan, rows, wide), BF16),
            pltpu.VMEM((rank_a, rows, wide), BF16),
            pltpu.VMEM((out_slots, out_step, rows, side), BF16),
            pltpu.VMEM((back_slots, chan, STEP, side), BF16),
            pltpu.VMEM((chan * STEP, rank_a * STEP), BF16),
            *[pltpu.VMEM(shape, F32) for shape in grads],
            pltpu.SemaphoreType.DMA((2,)),
            pltpu.SemaphoreType.DMA((out_steps,)),
            pltpu.SemaphoreType.DMA((2, 4)),
            pltpu.SemaphoreType.DMA((out_slots,)),
            pltpu.SemaphoreType.DMA((back_slots,)),
        ],
        compiler_params=params(60),
        name="output",
    )(first_t, table_t, out_rows, back_rows, g_first, g_second, g_third, g_fourth)

    return (
        output_field,
        input_grad,
        g_first.T,
        g_second.reshape(rank_a, rank_b, channels).transpose(0, 2, 1),
        g_third.transpose(0, 2, 1),
        g_fourth,
    )


def solution(mesh):
    placed = (P("chan", "grid", None), P("chan", "grid", None), P(), P(), P(), P())
    return jax.shard_map(
        local,
        mesh=mesh,
        in_specs=placed,
        out_specs=(P("chan", "grid", None), P("chan", "grid", None), P(), P(), P(), P()),
        check_vma=False,
    )
```

time: 132 us -> 102 us (0.77)
  local copies, waits for them, and re-layouts: 15.2 us -> 0 us
  Pallas kernels: 116 us -> 101 us
    pallas_call x4 -> x2, Pallas kernels: 116 us -> 101 us  [the longest x1 84.2 us: local(): pl.pallas_call(spectral_kernel, in_specs=[anywhere] * 3 + [vmem] * 5, out...]
    unnamed x33 -> x0, local copies, waits for them, and re-layouts: 11.2 us -> none
    dynamic_slice x3 -> x0, local copies, waits for them, and re-layouts: 3.09 us -> none  [the longest x1 1.66 us: local(): lax.dynamic_slice_in_dim(core_third.transpose(0, 2, 1), chan_index % 2 *...]
where the time goes in v2:
time: 102 us
  Pallas kernels  101 us (99%)
    pallas_call x1, Pallas kernels, local(): pl.pallas_call(spectral_kernel, in_specs=[anywhere] * 3 + [vmem] * 5, out...  84.2 us
    pallas_call x1, Pallas kernels, local(): pl.pallas_call(output_kernel, in_specs=[vmem] + [anywhere] * 7, out_specs...  16.9 us

profile of v2, /device:TPU:0, one launch (start us, length us, event | category | flops | bytes accessed | tf_op | source)
XLA Modules:
  0.0 101.7 jit_solution(92343468703619637)
XLA Ops:
  0.6 84.2 %spectral.1 = (bf16[64,128,256]{2,1,0:T(8,128)(2,1)}, bf16[16,128,256]{2,1,0:T(8,128)(2,1)}, f32[16,256]{1,0:T(8,128)}, f32[256,256]{1,0:T(8,128)}, f32[16,16,128]{2,1,0:T(8,128)}, /*index=5*/f32[2,16,128]{2,1,0:T(8,128)}) custom-call(bf16[64,128,1024]{2,1,0:T(8,128)(2,1)} %field.1, bf16[64,128,1024]{2,1,0:T(8,128)(2,1)} %cot.1, ...), custom_call_target="tpu_custom_call" | custom-call | tf_op jit(solution)/shard_map/spectral/pallas_call | solution.py:888
  84.8 16.9 %output.1 = (bf16[64,128,1024]{2,1,0:T(8,128)(2,1)}, bf16[64,128,1024]{2,1,0:T(8,128)(2,1)}, f32[16,256]{1,0:T(8,128)}, f32[256,256]{1,0:T(8,128)}, f32[16,16,128]{2,1,0:T(8,128)}, /*index=5*/f32[2,16,128]{2,1,0:T(8,128)}) custom-call(f32[16,256]{1,0:T(8,128)} %bitcast.13, bf16[256,1024]{1,0:T(8,128)(2,1)} %constant.7.clone.table_in, ...), custom_call_target="tpu_custom_call" | custom-call | tf_op jit(solution)/shard_map/output/pallas_call | solution.py:913

commit v3 on v2

--- a/solution.py
+++ b/solution.py
@@ -190,9 +190,9 @@
 
 
 def spectral_kernel(
-    field, cot, turns_in, table, first_t, second, third, column,
-    rows_out, back_rows, g_first, g_second, g_third, g_fourth,
-    block_v, modes_v, y, held, spec_stage, spec, s_stage, spec_out, cs, csf, csb, kron, mixed,
+    field, cot, turns_in, table_in, first_t, second, third, column,
+    rows_out, back_out, kron_out, g_first, g_second, g_third, g_fourth,
+    block_v, kron_back, table, back_rows, outer_a, outer_b, modes_v, y, held, spec_stage, spec, s_stage, spec_out, cs, csf, csb, kron, mixed,
     by_ab, by_ba, by_t, kern, lead_f, kgrad, outer, held_o, part_second, back_in, total,
     lead_v, lead_core, lead_x, lead_res, lead_lp, lead_ls, lead_mid,
     lg_x, lg_all, lg_lp, lg_ls, lg_mid,
@@ -200,7 +200,7 @@
     f_core, f_plane, f_stack,
     lead_send, lead_recv, lg_send, lg_recv, gp_send, gp_recv,
     core_send, core_recv, spec_send, spec_recv, out_send, out_recv, f_send, f_recv,
-    block_sem, turns_sem, rows_sem,
+    block_sem, turns_sem, rows_sem, wide_sem,
 ):
     if outer.shape[0] * outer.shape[1] * 2 < kern.shape[0]:
         outer = block_v
@@ -250,17 +250,17 @@
     peers = at.peers()
     for peer in peers:
         pl.semaphore_signal(barrier, inc=1, device_id=peer, device_id_type=MESH)
+    table_copy = pltpu.make_async_copy(table_in, table, turns_sem.at[1])
+    table_copy.start()
     for k in range(min(slots, 2 * subs)):
-        fetch(jnp.int32(k))
-    turns_copy = pltpu.make_async_copy(turns_in.at[at.grid], cs, turns_sem)
+        if k < subs:
+            block_copy(field, k, k).start()
+        else:
+            block_copy(cot, k - subs, k).start()
+    turns_copy = pltpu.make_async_copy(turns_in.at[at.grid], cs, turns_sem.at[0])
     turns_copy.start()
     kron[...] = spread(first_t[...].astype(BF16), ra, chan, at.chan * chan)
-    turns_copy.wait()
-    c, s = cs[0], cs[1]
-    csf[:mx, :n], csf[:mx, n:], csf[mx:, :n], csf[mx:, n:] = c, s, -s, c
-    ct = jnp.swapaxes(c.astype(F32), 0, 1).astype(BF16)
-    st = jnp.swapaxes(s.astype(F32), 0, 1).astype(BF16)
-    csb[:n, :mx], csb[:n, mx:], csb[n:, :mx], csb[n:, mx:] = ct, -st, st, ct
+    table_copy.wait()
 
     mixed[...] = jnp.zeros_like(mixed)
 
@@ -277,6 +277,12 @@
         return carry
 
     lax.fori_loop(0, subs, field_body, 0)
+    turns_copy.wait()
+    c, s = cs[0], cs[1]
+    csf[:mx, :n], csf[:mx, n:], csf[mx:, :n], csf[mx:, n:] = c, s, -s, c
+    ct = jnp.swapaxes(c.astype(F32), 0, 1).astype(BF16)
+    st = jnp.swapaxes(s.astype(F32), 0, 1).astype(BF16)
+    csb[:n, :mx], csb[:n, mx:], csb[n:, :mx], csb[n:, mx:] = ct, -st, st, ct
     for g in range(row_groups):
         for q in range(2):
             for a in range(ra):
@@ -334,8 +340,7 @@
     lead_core_copy().wait()
     mine = lead_v[pl.ds(core * half, half)].astype(F32) + lead_core[...].astype(F32)
     lead_x[...] = mine.reshape(lead_x.shape).astype(BF16)
-    for r in lead_sums:
-        r.plane_send()
+    lead_sums[0].plane_send()
 
     def plan(hooks, index):
         for when, todo in hooks:
@@ -359,9 +364,16 @@
         return [one] + ([two] if split else [])
 
     cot_hooks = [
-        (min(1, subs - 1), [first_lead.plane_wait, first_lead.stack_send]),
-        (min(2, subs - 1), [last_lead.plane_wait, last_lead.stack_send] if split else []),
-        (min(3, subs - 1), [first_lead.stack_wait, first_lead.stack_back_send]),
+        (
+            min(1, subs - 1),
+            [first_lead.plane_wait, first_lead.stack_send]
+            + ([last_lead.plane_send] if split else []),
+        ),
+        (
+            min(3, subs - 1),
+            [first_lead.stack_wait, first_lead.stack_back_send]
+            + ([last_lead.plane_wait, last_lead.stack_send] if split else []),
+        ),
     ]
 
     def cot_body(i, carry):
@@ -413,9 +425,13 @@
     back_hooks = []
     if split:
         back_hooks = [
-            (rounds // 4, [last_lead.stack_wait, last_lead.stack_back_send]),
-            (rounds // 2, [first_lg.plane_send]),
-            (rounds * 3 // 4, [first_lead.stack_back_wait, first_lead.plane_back_send]),
+            (
+                rounds * 11 // 16,
+                [
+                    first_lead.stack_back_wait, first_lead.plane_back_send,
+                    last_lead.stack_wait, last_lead.stack_back_send, first_lg.plane_send,
+                ],
+            ),
         ]
     lax.fori_loop(0, rounds, back_body, 0)
     last_lg.plane_send()
@@ -431,9 +447,7 @@
         if folded:
             lanes += row // (pairs // 2) * per * wide
             row %= pairs // 2
-        outer[j // outer.shape[1], j % outer.shape[1], row : row + rb, lanes : lanes + my] = (
-            value.astype(BF16)
-        )
+        outer[j // outer.shape[1], j % outer.shape[1], row : row + rb, lanes : lanes + my] = value
 
     def outer_get(j, lanes, size):
         slab = outer.at[j // outer.shape[1], j % outer.shape[1]]
@@ -443,7 +457,13 @@
         high = slab[:, per * wide + lanes : per * wide + lanes + size]
         return jnp.concatenate([low, high], axis=0)
 
-    def mix_body(j, carry):
+    outer_b[...] = jnp.zeros_like(outer_b)
+
+    def add_second(kept, j):
+        rhs = jnp.concatenate([spec[j * per + u] for u in range(per)], axis=1)
+        part_second[...] += dot_nt(kept[...], rhs)
+
+    def products(j, kept):
         for u in range(per):
             k = j * per + u
             g = dot(by_ab[...], spec[k])
@@ -454,35 +474,43 @@
             for a in range(ra):
                 rows = slice(a * rb, (a + 1) * rb)
                 lre, lim = lead_f[k, a : a + 1, :my], lead_f[k, a : a + 1, my:]
-                outer_put(j, a, u * wide, kre * lre - kim * lim)
-                outer_put(j, a, u * wide + my, kre * lim + kim * lre)
+                ore = (kre * lre - kim * lim).astype(BF16)
+                oim = (kre * lim + kim * lre).astype(BF16)
+                kept[rows, u * wide : u * wide + my] = ore
+                kept[rows, u * wide + my : (u + 1) * wide] = oim
+                outer_put(j, a, u * wide, ore)
+                outer_put(j, a, u * wide + my, oim)
                 gre, gim = g[rows, :my], g[rows, my:]
                 re += gre * lre + gim * lim
                 im += gim * lre - gre * lim
             at_k = pl.ds(pl.multiple_of(k * rb, rb), rb)
             kgrad[at_k, :my] = re
             kgrad[at_k, my:] = im
-        rhs = jnp.concatenate([spec[j * per + u] for u in range(per)], axis=1)
-        part_second[...] += dot_nt(outer_get(j, 0, per * wide), rhs)
-
-        plan(mix_hooks, j)
+
+    def mix_body(i, carry):
+        add_second(outer_b, jnp.maximum(2 * i - 1, 0))
+        products(2 * i, outer_a)
+        add_second(outer_a, 2 * i)
+        products(2 * i + 1, outer_b)
+        plan(mix_hooks, i)
         return carry
 
-    turns_of_part = half // per // parts
+    turns_of_part = half // per // parts // 2
+    tp = turns_of_part
     if split:
         mix_hooks = [
-            (turns_of_part // 4, [first_lg.plane_wait, first_lg.stack_send]),
-            (turns_of_part // 2, [last_lg.plane_wait, last_lg.stack_send]),
-            (turns_of_part * 3 // 4, [first_lg.stack_wait, first_lg.stack_back_send]),
-            (turns_of_part * 9 // 8, [last_lg.stack_wait, last_lg.stack_back_send]),
-            (turns_of_part * 5 // 4, [first_lg.stack_back_wait, first_lg.plane_back_send]),
-            (turns_of_part * 13 // 8, [last_lg.stack_back_wait, last_lg.plane_back_send]),
+            (tp // 4, [first_lg.plane_wait, first_lg.stack_send]),
+            (tp * 5 // 8, [last_lg.plane_wait, last_lg.stack_send]),
+            (tp * 7 // 8, [first_lg.stack_wait, first_lg.stack_back_send]),
+            (tp + tp * 2 // 8, [last_lg.stack_wait, last_lg.stack_back_send]),
+            (tp + tp * 4 // 8, [first_lg.stack_back_wait, first_lg.plane_back_send]),
+            (tp + tp * 7 // 8, [last_lg.stack_back_wait, last_lg.plane_back_send]),
         ]
     else:
         mix_hooks = [
-            (turns_of_part // 8, [last_lg.plane_wait, last_lg.stack_send]),
-            (turns_of_part * 3 // 8, [last_lg.stack_wait, last_lg.stack_back_send]),
-            (turns_of_part * 7 // 8, [last_lg.stack_back_wait, last_lg.plane_back_send]),
+            (tp // 8, [last_lg.plane_wait, last_lg.stack_send]),
+            (tp * 3 // 8, [last_lg.stack_wait, last_lg.stack_back_send]),
+            (tp * 7 // 8, [last_lg.stack_back_wait, last_lg.plane_back_send]),
         ]
     for p in range(parts):
         share = half // parts
@@ -492,6 +520,7 @@
         lead_f[p * share : (p + 1) * share, :, :my] = got[:, 0]
         lead_f[p * share : (p + 1) * share, :, my:] = got[:, 1]
         lax.fori_loop(p * turns_of_part, (p + 1) * turns_of_part, mix_body, 0)
+    add_second(outer_b, half // per - 1)
 
     def second_copy():
         return remote(
@@ -499,19 +528,29 @@
             core_send.at[1], core_recv.at[1], partner,
         )
 
-    def back_copy():
-        return remote(lg_all.at[core], lg_all.at[core], core_send.at[2], core_recv.at[2], partner)
+    def back_copy(p):
+        where = pl.ds(p * (lg_all.shape[1] // parts), lg_all.shape[1] // parts)
+        return remote(
+            lg_all.at[core, where], lg_all.at[core, where],
+            core_send.at[5 + p], core_recv.at[5 + p], partner,
+        )
 
     second_copy().start()
     by_mode = jnp.swapaxes(kgrad[...].reshape(half, rb, wide), 0, 1).reshape(rb * half, wide)
-    part_third = dot_nt(col, by_mode, HI)
+    by_mode = by_mode.astype(BF16)
+    part_third = dot_nt(col.astype(BF16), by_mode)
     third_flat = jnp.concatenate(
         [jnp.where(core == 0, third[b][:, :half], third[b][:, half:]) for b in range(rb)], axis=1
     )
-    part_fourth = dot(third_flat, by_mode, HI)
+    part_fourth = dot(third_flat.astype(BF16), by_mode)
     second_copy().wait()
     mine = part_second[pl.ds(core * (pairs // 2), pairs // 2)] + gp_core[...]
-    mine = dot(mine, one_hot(both, channels, at.chan // 2 * both).astype(F32), HI)
+    if both % LANES:
+        mine = dot(mine, one_hot(both, channels, at.chan // 2 * both).astype(F32), HI)
+    else:
+        mine = jnp.concatenate(
+            [jnp.where(at.chan // 2 == p, mine, 0.0) for p in range(channels // both)], axis=1
+        )
 
     pieces = []
     for value in (mine, part_third, part_fourth):
@@ -528,11 +567,51 @@
     if count < gp_x.shape[0]:
         gp_x[count:] = jnp.zeros((gp_x.shape[0] - count, 8, LANES), F32)
     gp_sum.plane_send()
-    for r in lg_sums:
-        r.plane_back_wait()
-    back_copy().start()
-
-    back_copy().wait()
+    if split:
+        first_lg.plane_back_wait()
+        back_copy(0).start()
+    pick = one_hot(chan, channels, at.chan * chan).astype(BF16)
+    first_bf = dot_nt(pick, first_t[...].astype(BF16)).astype(BF16)
+    kron_back[...] = spread(first_bf, chan, ra)
+    kron_copy = pltpu.make_async_copy(kron_back, kron_out, turns_sem.at[3])
+    kron_copy.start()
+
+    groups = half // STEP
+
+    def out_copy(g):
+        return remote(
+            s_stage.at[g, :, :, pl.ds(other * chan * my, chan * my)],
+            spec_out.at[:, pl.ds(core * half + g * STEP, STEP), :],
+            out_send.at[g], out_recv.at[g], partner,
+        )
+
+    def out_body(g, carry):
+        for j in range(STEP // per):
+            for u in range(per):
+                held_o[j * per + u, :both] = dot(
+                    by_t[...], outer_get(g * (STEP // per) + j, u * wide, wide)
+                )
+        turned = jnp.swapaxes(held_o[:, :both], 0, 1).astype(BF16)
+        for o in range(both):
+            for q in range(2):
+                s_stage[g, q, :, o * my : (o + 1) * my] = turned[o, :, q * my : (q + 1) * my]
+        out_copy(g).start()
+        row = pl.ds(pl.multiple_of(core * half + g * STEP, STEP), STEP)
+        lanes = pl.ds(pl.multiple_of(core * chan * my, chan * my), chan * my)
+        spec_out[:, row, :] = s_stage[g, :, :, lanes]
+
+        @pl.when(g == groups - 1)
+        def _():
+            gp_sum.plane_wait()
+            gp_sum.stack_send()
+
+        return carry
+
+    lax.fori_loop(0, groups, out_body, 0)
+    last_lg.plane_back_wait()
+    back_copy(parts - 1).start()
+    for p in range(parts):
+        back_copy(p).wait()
     for q in range(2):
         for h in range(2):
             got = lg_all[h].reshape(half, 2, ra, my)[:, q].astype(F32)
@@ -599,45 +678,6 @@
             first_stack_copy(s).start()
 
     first_core_copy().start()
-    gp_sum.plane_wait()
-    gp_sum.stack_send()
-
-    def out_copy(g):
-        return remote(
-            s_stage.at[g, :, :, pl.ds(other * chan * my, chan * my)],
-            spec_out.at[:, pl.ds(core * half + g * STEP, STEP), :],
-            out_send.at[g], out_recv.at[g], partner,
-        )
-
-    def out_body(g, carry):
-        for j in range(STEP // per):
-            for u in range(per):
-                held_o[j * per + u, :both] = dot(
-                    by_t[...], outer_get(g * (STEP // per) + j, u * wide, wide)
-                )
-        turned = jnp.swapaxes(held_o[:, :both], 0, 1).astype(BF16)
-        for o in range(both):
-            for q in range(2):
-                s_stage[g, q, :, o * my : (o + 1) * my] = turned[o, :, q * my : (q + 1) * my]
-        out_copy(g).start()
-        row = pl.ds(pl.multiple_of(core * half + g * STEP, STEP), STEP)
-        lanes = pl.ds(pl.multiple_of(core * chan * my, chan * my), chan * my)
-        spec_out[:, row, :] = s_stage[g, :, :, lanes]
-
-        @pl.when(g == 0)
-        def _():
-            first_plane()
-
-        @pl.when(g == 2)
-        def _():
-            gp_sum.stack_wait()
-            gp_sum.stack_back_send()
-            first_stack()
-
-        return carry
-
-    groups = half // STEP
-    lax.fori_loop(0, groups, out_body, 0)
     for g in range(groups):
         out_copy(g).wait()
 
@@ -656,15 +696,32 @@
                 modes_v[i * turns + c, :, q * my : (q + 1) * my] = part.astype(BF16)
         rows_copy(i).start()
 
-        @pl.when(i == 0)
+        @pl.when(i == steps // 4)
         def _():
-            gp_sum.stack_back_wait()
-            gp_sum.plane_back_send()
+            gp_sum.stack_wait()
+            gp_sum.stack_back_send()
+            first_plane()
 
         return carry
 
     steps = chan // turns
     lax.fori_loop(0, steps, rows_body, 0)
+    first_stack()
+    gp_sum.stack_back_wait()
+    gp_sum.plane_back_send()
+
+    def wide_copy(i):
+        where = pl.ds(i * 4, 4)
+        return pltpu.make_async_copy(block_v.at[0, where], back_out.at[where], wide_sem.at[i])
+
+    def wide_body(i, carry):
+        part = back_rows[pl.ds(i * 4, 4)].reshape(4 * n, wide)
+        product = dot_nt(part, table[...]) * (1.0 / side)
+        block_v[0, pl.ds(i * 4, 4)] = product.astype(BF16).reshape(4, n, side)
+        wide_copy(i).start()
+        return carry
+
+    lax.fori_loop(0, ra // 4, wide_body, 0)
     for s in range(1, at.stacks):
         first_stack_copy(s).wait()
     value = f_stack[0]
@@ -698,16 +755,19 @@
         g_fourth[q] = tile(0, cols + rb // 2 + q) + tile(1, cols + rb // 2 + q)
     for i in range(steps):
         rows_copy(i).wait()
+    kron_copy.wait()
+    for i in range(ra // 4):
+        wide_copy(i).wait()
 
 
 def output_kernel(
-    first_t, table_in, rows_in, back_in, *refs
+    table_in, rows_in, back_in, kron_in, *refs
 ):
     grads_in, (out, out_back), grads_out = refs[:4], refs[4:6], refs[6:10]
     table, rows, back, out_v, back_v, kron = refs[10:16]
     grads, (in_sem, rows_sem, grad_sem, out_sem, back_sem) = refs[16:20], refs[20:]
     chan, n, side = out.shape
-    rank, _, wide = back.shape
+    rank, wide = back.shape[0], rows.shape[2]
     slots, block = out_v.shape[:2]
     steps, row_steps = chan // block, n // STEP
     back_slots = back_v.shape[0]
@@ -721,12 +781,11 @@
     table_copy.start()
     for i in range(steps):
         rows_copy(i).start()
+    kron_copy = pltpu.make_async_copy(kron_in, kron, in_sem.at[2])
+    kron_copy.start()
     back_copy.start()
     for i in range(4):
         pltpu.make_async_copy(grads_in[i], grads[i], grad_sem.at[0, i]).start()
-    pick = one_hot(chan, first_t.shape[1], lax.axis_index("chan") * chan).astype(BF16)
-    first = dot_nt(pick, first_t[...].astype(BF16)).astype(BF16)
-    kron[...] = spread(first, chan, rank)
 
     def out_copy(i):
         slot = lax.rem(i, slots)
@@ -759,15 +818,15 @@
         def _():
             in_copy(i - back_slots).wait()
 
-        part = back[:, pl.ds(pl.multiple_of(i * STEP, STEP), STEP), :].reshape(rank * STEP, wide)
-        mid = (dot(kron[...], part) * (1.0 / side)).astype(BF16)
-        product = dot(mid, table[...])
+        part = back[:, pl.ds(pl.multiple_of(i * STEP, STEP), STEP), :].reshape(rank * STEP, side)
+        product = dot(kron[...], part)
         back_v[lax.rem(i, back_slots)] = product.astype(BF16).reshape(chan, STEP, side)
         in_copy(i).start()
         return carry
 
     table_copy.wait()
     lax.fori_loop(0, steps, out_body, 0)
+    kron_copy.wait()
     back_copy.wait()
     for i in range(4):
         pltpu.make_async_copy(grads_in[i], grads[i], grad_sem.at[0, i]).wait()
@@ -836,6 +895,11 @@
     tile = (rank_a, modes_y)
     scratch = [
         pltpu.VMEM((slots, sub, rows, side), BF16),
+        pltpu.VMEM((chan * STEP, rank_a * STEP), BF16),
+        pltpu.VMEM((side, wide), BF16),
+        pltpu.VMEM((rank_a, rows, wide), BF16),
+        pltpu.VMEM((pairs, 2 * wide), BF16),
+        pltpu.VMEM((pairs, 2 * wide), BF16),
         pltpu.VMEM((chan, rows, wide), BF16),
         pltpu.VMEM((max(2 * rows, sub * STEP), wide_y), BF16),
         pltpu.VMEM((STEP, 2 * modes_x, modes_y), F32),
@@ -876,22 +940,24 @@
         pltpu.VMEM((stacks, rank_a, channels), F32),
         *[pltpu.SemaphoreType.DMA((parts, 4, peers))] * 4,
         *[pltpu.SemaphoreType.DMA((4, peers))] * 2,
-        *[pltpu.SemaphoreType.DMA((5,))] * 2,
+        *[pltpu.SemaphoreType.DMA((5 + parts,))] * 2,
         *[pltpu.SemaphoreType.DMA((blocks,))] * 2,
         *[pltpu.SemaphoreType.DMA((groups,))] * 2,
         *[pltpu.SemaphoreType.DMA((2, peers))] * 2,
         pltpu.SemaphoreType.DMA((slots,)),
-        pltpu.SemaphoreType.DMA,
+        pltpu.SemaphoreType.DMA((4,)),
         pltpu.SemaphoreType.DMA((steps,)),
+        pltpu.SemaphoreType.DMA((rank_a // 4,)),
     ]
     vmem = pl.BlockSpec(memory_space=pltpu.VMEM)
-    out_rows, back_rows, g_first, g_second, g_third, g_fourth = pl.pallas_call(
+    out_rows, back_rows, kron, g_first, g_second, g_third, g_fourth = pl.pallas_call(
         spectral_kernel,
-        in_specs=[anywhere] * 3 + [vmem] * 5,
-        out_specs=[anywhere] + [vmem] * 5,
+        in_specs=[anywhere] * 4 + [vmem] * 4,
+        out_specs=[anywhere] * 3 + [vmem] * 4,
         out_shape=[
             jax.ShapeDtypeStruct((chan, rows, wide), BF16),
-            jax.ShapeDtypeStruct((rank_a, rows, wide), BF16),
+            jax.ShapeDtypeStruct((rank_a, rows, side), BF16),
+            jax.ShapeDtypeStruct((chan * STEP, rank_a * STEP), BF16),
             jax.ShapeDtypeStruct((rank_a, channels), F32),
             jax.ShapeDtypeStruct((pairs, channels), F32),
             jax.ShapeDtypeStruct((rank_b, rank_d, modes_x), F32),
@@ -912,7 +978,7 @@
     ]
     output_field, input_grad, g_first, g_second, g_third, g_fourth = pl.pallas_call(
         output_kernel,
-        in_specs=[vmem] + [anywhere] * 7,
+        in_specs=[anywhere] * 8,
         out_specs=[anywhere] * 6,
         out_shape=[
             jax.ShapeDtypeStruct((chan, rows, side), BF16),
@@ -922,12 +988,12 @@
         scratch_shapes=[
             pltpu.VMEM((wide, side), BF16),
             pltpu.VMEM((chan, rows, wide), BF16),
-            pltpu.VMEM((rank_a, rows, wide), BF16),
+            pltpu.VMEM((rank_a, rows, side), BF16),
             pltpu.VMEM((out_slots, out_step, rows, side), BF16),
             pltpu.VMEM((back_slots, chan, STEP, side), BF16),
             pltpu.VMEM((chan * STEP, rank_a * STEP), BF16),
             *[pltpu.VMEM(shape, F32) for shape in grads],
-            pltpu.SemaphoreType.DMA((2,)),
+            pltpu.SemaphoreType.DMA((3,)),
             pltpu.SemaphoreType.DMA((out_steps,)),
             pltpu.SemaphoreType.DMA((2, 4)),
             pltpu.SemaphoreType.DMA((out_slots,)),
@@ -935,7 +1001,7 @@
         ],
         compiler_params=params(60),
         name="output",
-    )(first_t, table_t, out_rows, back_rows, g_first, g_second, g_third, g_fourth)
+    )(table_t, out_rows, back_rows, kron, g_first, g_second, g_third, g_fourth)
 
     return (
         output_field,

time: 102 us -> 95.1 us (0.932)
  Pallas kernels: 101 us -> 94.3 us
    pallas_call x2, Pallas kernels: 101 us -> 94.3 us  [the longest x1 79.4 us: local(): pl.pallas_call(spectral_kernel, in_specs=[anywhere] * 4 + [vmem] * 4, out...]
where the time goes in v3:
time: 95.1 us; the launch traced here: 94.9 us
  Pallas kernels  94.3 us (99%)
    pallas_call x1, Pallas kernels, local(): pl.pallas_call(spectral_kernel, in_specs=[anywhere] * 4 + [vmem] * 4, out...  79.4 us
    pallas_call x1, Pallas kernels, local(): pl.pallas_call(output_kernel, in_specs=[anywhere] * 8, out_specs=[anywher...  14.9 us

profile of v3, /device:TPU:0, one launch (start us, length us, event | category | flops | bytes accessed | tf_op | source)
XLA Modules:
  0.0 94.9 jit_solution(11472357434838898026)
XLA Ops:
  0.6 79.4 %spectral.1 = (bf16[64,128,256]{2,1,0:T(8,128)(2,1)}, bf16[16,128,1024]{2,1,0:T(8,128)(2,1)}, bf16[1024,256]{1,0:T(8,128)(2,1)}, f32[16,256]{1,0:T(8,128)}, f32[...) custom-call(bf16[64,128,1024]{2,1,0:T(8,128)(2,1)} %field.1, bf16[64,128,1024]{2,1,0:T(8,128)(2,1)} %cot.1, ...), custom_call_target="tpu_custom_call" | custom-call | tf_op jit(solution)/shard_map/spectral/pallas_call | solution.py:953
  80.1 14.9 %output.1 = (bf16[64,128,1024]{2,1,0:T(8,128)(2,1)}, bf16[64,128,1024]{2,1,0:T(8,128)(2,1)}, f32[16,256]{1,0:T(8,128)}, f32[256,256]{1,0:T(8,128)}, f32[16,16,128]{2,1,0:T(8,128)}, /*index=5*/f32[2,16,128]{2,1,0:T(8,128)}) custom-call(bf16[256,1024]{1,0:T(8,128)(2,1)} %constant.7.clone.table_in, bf16[64,128,256]{2,1,0:T(8,128)(2,1)} %get-tuple-element.19.rows_in, ...), custom_call_target="tpu_custom_call" | custom-call | tf_op jit(solution)/shard_map/output/pallas_call | solution.py:979

commit v4 on v3

--- a/solution.py
+++ b/solution.py
@@ -109,12 +109,11 @@
 
 
 class Reduce:
-    def __init__(self, place, source, result, land_plane, land_stack, mid, send, recv):
+    def __init__(self, place, source, result, land_plane, land_stack, send, recv):
         self.at, self.source, self.result = place, source, result
-        self.land_plane, self.land_stack, self.mid = land_plane, land_stack, mid
+        self.land_plane, self.land_stack = land_plane, land_stack
         self.send, self.recv = send, recv
         self.chunk = source.shape[0] // place.planes
-        self.piece = self.chunk // place.stacks
 
     def plane_copy(self, s):
         there = flip(self.at.plane, s)
@@ -134,13 +133,64 @@
         total = self.source[pl.ds(self.at.plane * self.chunk, self.chunk)].astype(F32)
         for s in range(1, self.at.planes):
             total = total + self.land_plane[s - 1].astype(F32)
+        self.keep(total)
+
+    def keep(self, total):
+        self.land_stack[self.at.stack] = total.astype(self.land_stack.dtype)
+
+    def stack_copy(self, s):
+        mine = self.land_stack.at[self.at.stack]
+        return remote(
+            mine, mine, self.send.at[1, s - 1], self.recv.at[1, s - 1], self.at.across_stack(s)
+        )
+
+    def stack_send(self):
+        for s in range(1, self.at.stacks):
+            self.stack_copy(s).start()
+
+    def stack_wait(self):
+        for s in range(1, self.at.stacks):
+            self.stack_copy(s).wait()
+        total = self.land_stack[0].astype(F32)
+        for s in range(1, self.at.stacks):
+            total = total + self.land_stack[s].astype(F32)
+        here = pl.ds(self.at.plane * self.chunk, self.chunk)
+        self.result[here] = total.astype(self.result.dtype)
+
+    def plane_back_copy(self, s):
+        here = pl.ds(self.at.plane * self.chunk, self.chunk)
+        return remote(
+            self.result.at[here], self.result.at[here],
+            self.send.at[2, s - 1], self.recv.at[2, s - 1], self.at.across_plane(s),
+        )
+
+    def plane_back_send(self):
+        for s in range(1, self.at.planes):
+            self.plane_back_copy(s).start()
+
+    def plane_back_wait(self):
+        for s in range(1, self.at.planes):
+            self.plane_back_copy(s).wait()
+
+
+class ScatterReduce(Reduce):
+    def __init__(self, place, source, result, land_plane, land_stack, send, recv):
+        super().__init__(place, source, result, land_plane, land_stack, send, recv)
+        self.piece = self.chunk // place.stacks
+        self.mid = land_stack.at[0]
+        self.land_stack = [
+            land_stack.at[1 + s // place.stacks, pl.ds(s % place.stacks * self.piece, self.piece)]
+            for s in range(place.stacks - 1)
+        ]
+
+    def keep(self, total):
         self.mid[...] = total.astype(self.mid.dtype)
 
     def stack_copy(self, s):
         there = flip(self.at.stack, s)
         return remote(
             self.mid.at[pl.ds(there * self.piece, self.piece)],
-            self.land_stack.at[s - 1],
+            self.land_stack[s - 1],
             self.send.at[1, s - 1], self.recv.at[1, s - 1], self.at.across_stack(s),
         )
 
@@ -156,13 +206,13 @@
             self.stack_copy(s).wait()
         total = self.mid[pl.ds(self.at.stack * self.piece, self.piece)].astype(F32)
         for s in range(1, self.at.stacks):
-            total = total + self.land_stack[s - 1].astype(F32)
+            total = total + self.land_stack[s - 1][...].astype(F32)
         self.result[self.own()] = total.astype(self.result.dtype)
 
     def stack_back_copy(self, s):
         return remote(
             self.result.at[self.own()], self.result.at[self.own()],
-            self.send.at[2, s - 1], self.recv.at[2, s - 1], self.at.across_stack(s),
+            self.send.at[3, s - 1], self.recv.at[3, s - 1], self.at.across_stack(s),
         )
 
     def stack_back_send(self):
@@ -172,21 +222,6 @@
     def stack_back_wait(self):
         for s in range(1, self.at.stacks):
             self.stack_back_copy(s).wait()
-
-    def plane_back_copy(self, s):
-        here = pl.ds(self.at.plane * self.chunk, self.chunk)
-        return remote(
-            self.result.at[here], self.result.at[here],
-            self.send.at[3, s - 1], self.recv.at[3, s - 1], self.at.across_plane(s),
-        )
-
-    def plane_back_send(self):
-        for s in range(1, self.at.planes):
-            self.plane_back_copy(s).start()
-
-    def plane_back_wait(self):
-        for s in range(1, self.at.planes):
-            self.plane_back_copy(s).wait()
 
 
 def spectral_kernel(
@@ -194,9 +229,9 @@
     rows_out, back_out, kron_out, g_first, g_second, g_third, g_fourth,
     block_v, kron_back, table, back_rows, outer_a, outer_b, modes_v, y, held, spec_stage, spec, s_stage, spec_out, cs, csf, csb, kron, mixed,
     by_ab, by_ba, by_t, kern, lead_f, kgrad, outer, held_o, part_second, back_in, total,
-    lead_v, lead_core, lead_x, lead_res, lead_lp, lead_ls, lead_mid,
-    lg_x, lg_all, lg_lp, lg_ls, lg_mid,
-    gp_core, gp_x, gp_all, gp_lp, gp_ls, gp_mid,
+    lead_v, lead_core, lead_x, lead_res, lead_lp, lead_ls,
+    lg_x, lg_all, lg_lp, lg_ls,
+    gp_core, gp_x, gp_all, gp_lp, gp_ls,
     f_core, f_plane, f_stack,
     lead_send, lead_recv, lg_send, lg_recv, gp_send, gp_recv,
     core_send, core_recv, spec_send, spec_recv, out_send, out_recv, f_send, f_recv,
@@ -318,24 +353,26 @@
     own_half = pl.ds(pl.multiple_of(core * half, half), half)
     kern[...] = jnp.swapaxes(held_o[:, own_half, :], 0, 1)
 
-    def sums(source, result, land_plane, land_stack, mid, send, recv):
+    split = parts > 1
+
+    def sums(kind, source, result, land_plane, land_stack, send, recv):
         share = source.shape[0] // parts
         made = []
         for p in range(parts):
             where = pl.ds(p * share, share)
-            made.append(Reduce(
+            made.append(kind(
                 at, source.at[where], result(where), land_plane.at[p], land_stack.at[p],
-                mid.at[p], send.at[p], recv.at[p],
+                send.at[p], recv.at[p],
             ))
         return made
 
     lead_sums = sums(
-        lead_x, lambda w: lead_res.at[w], lead_lp, lead_ls, lead_mid, lead_send, lead_recv
+        Reduce, lead_x, lambda w: lead_res.at[w], lead_lp, lead_ls, lead_send, lead_recv
     )
     lg_sums = sums(
-        lg_x, lambda w: lg_all.at[core, w], lg_lp, lg_ls, lg_mid, lg_send, lg_recv
+        ScatterReduce if split else Reduce, lg_x, lambda w: lg_all.at[core, w], lg_lp, lg_ls, lg_send, lg_recv
     )
-    gp_sum = Reduce(at, gp_x, gp_all.at[core], gp_lp, gp_ls, gp_mid, gp_send, gp_recv)
+    gp_sum = Reduce(at, gp_x, gp_all.at[core], gp_lp, gp_ls, gp_send, gp_recv)
 
     lead_core_copy().wait()
     mine = lead_v[pl.ds(core * half, half)].astype(F32) + lead_core[...].astype(F32)
@@ -358,7 +395,6 @@
 
     first_lead, last_lead = lead_sums[0], lead_sums[-1]
     first_lg, last_lg = lg_sums[0], lg_sums[-1]
-    split = parts > 1
 
     def both_of(one, two):
         return [one] + ([two] if split else [])
@@ -371,8 +407,7 @@
         ),
         (
             min(3, subs - 1),
-            [first_lead.stack_wait, first_lead.stack_back_send]
-            + ([last_lead.plane_wait, last_lead.stack_send] if split else []),
+            [last_lead.plane_wait, last_lead.stack_send] if split else [],
         ),
     ]
 
@@ -425,18 +460,13 @@
     back_hooks = []
     if split:
         back_hooks = [
-            (
-                rounds * 11 // 16,
-                [
-                    first_lead.stack_back_wait, first_lead.plane_back_send,
-                    last_lead.stack_wait, last_lead.stack_back_send, first_lg.plane_send,
-                ],
-            ),
+            (rounds * 6 // 16, [first_lead.stack_wait, first_lead.plane_back_send]),
+            (rounds * 11 // 16, [first_lg.plane_send]),
         ]
     lax.fori_loop(0, rounds, back_body, 0)
+    last_lead.stack_wait()
+    last_lead.plane_back_send()
     last_lg.plane_send()
-    last_lead.stack_back_wait()
-    last_lead.plane_back_send()
     part_second[...] = jnp.zeros_like(part_second)
 
     per = 2
@@ -499,18 +529,16 @@
     tp = turns_of_part
     if split:
         mix_hooks = [
-            (tp // 4, [first_lg.plane_wait, first_lg.stack_send]),
-            (tp * 5 // 8, [last_lg.plane_wait, last_lg.stack_send]),
-            (tp * 7 // 8, [first_lg.stack_wait, first_lg.stack_back_send]),
-            (tp + tp * 2 // 8, [last_lg.stack_wait, last_lg.stack_back_send]),
-            (tp + tp * 4 // 8, [first_lg.stack_back_wait, first_lg.plane_back_send]),
-            (tp + tp * 7 // 8, [last_lg.stack_back_wait, last_lg.plane_back_send]),
+            (tp * 6 // 8, [first_lg.plane_wait, first_lg.stack_send]),
+            (tp + tp // 8, [last_lg.plane_wait, last_lg.stack_send]),
+            (tp + tp * 3 // 8, [first_lg.stack_wait, first_lg.stack_back_send]),
+            (tp + tp * 5 // 8, [last_lg.stack_wait, last_lg.stack_back_send]),
+            (tp + tp * 7 // 8, [first_lg.stack_back_wait, first_lg.plane_back_send]),
         ]
     else:
         mix_hooks = [
-            (tp // 8, [last_lg.plane_wait, last_lg.stack_send]),
-            (tp * 3 // 8, [last_lg.stack_wait, last_lg.stack_back_send]),
-            (tp * 7 // 8, [last_lg.stack_back_wait, last_lg.plane_back_send]),
+            (tp // 4, [last_lg.plane_wait, last_lg.stack_send]),
+            (tp * 7 // 8, [last_lg.stack_wait, last_lg.plane_back_send]),
         ]
     for p in range(parts):
         share = half // parts
@@ -558,18 +586,18 @@
             pieces.append((value, c))
     spots, count = [], 0
     for value, c in pieces:
-        tiles = value.shape[0] // 8
-        gp_x[count : count + tiles] = value[:, c * LANES : (c + 1) * LANES].reshape(
-            tiles, 8, LANES
+        tiles = value.shape[0] // STEP
+        gp_x[count : count + tiles] = value[:, c * LANES : (c + 1) * LANES].astype(BF16).reshape(
+            tiles, STEP, LANES
         )
         spots.append((count, tiles))
         count += tiles
     if count < gp_x.shape[0]:
-        gp_x[count:] = jnp.zeros((gp_x.shape[0] - count, 8, LANES), F32)
+        gp_x[count:] = jnp.zeros((gp_x.shape[0] - count, STEP, LANES), BF16)
     gp_sum.plane_send()
     if split:
-        first_lg.plane_back_wait()
-        back_copy(0).start()
+        last_lg.stack_back_wait()
+        last_lg.plane_back_send()
     pick = one_hot(chan, channels, at.chan * chan).astype(BF16)
     first_bf = dot_nt(pick, first_t[...].astype(BF16)).astype(BF16)
     kron_back[...] = spread(first_bf, chan, ra)
@@ -600,10 +628,16 @@
         lanes = pl.ds(pl.multiple_of(core * chan * my, chan * my), chan * my)
         spec_out[:, row, :] = s_stage[g, :, :, lanes]
 
-        @pl.when(g == groups - 1)
+        @pl.when(g == groups // 2)
         def _():
             gp_sum.plane_wait()
             gp_sum.stack_send()
+
+        if split:
+            @pl.when(g == groups - 1)
+            def _():
+                first_lg.plane_back_wait()
+                back_copy(0).start()
 
         return carry
 
@@ -698,17 +732,18 @@
 
         @pl.when(i == steps // 4)
         def _():
+            first_plane()
+
+        @pl.when(i == steps * 5 // 8)
+        def _():
             gp_sum.stack_wait()
-            gp_sum.stack_back_send()
-            first_plane()
+            gp_sum.plane_back_send()
 
         return carry
 
     steps = chan // turns
     lax.fori_loop(0, steps, rows_body, 0)
     first_stack()
-    gp_sum.stack_back_wait()
-    gp_sum.plane_back_send()
 
     def wide_copy(i):
         where = pl.ds(i * 4, 4)
@@ -738,7 +773,7 @@
 
     def tile(h, index):
         start, size = spots[index]
-        return gp_all[h, start : start + size].reshape(size * 8, LANES) * (1.0 / mx)
+        return gp_all[h, start : start + size].reshape(size * STEP, LANES).astype(F32) * (1.0 / mx)
 
     cols = channels // LANES
     for h in range(2):
@@ -869,8 +904,8 @@
     planes, stacks = chan_count, grid_count // 2
     tiles = 2 * half
     owners = planes * stacks
-    grad_tiles = (pairs // 2 * channels + rank_d * rank_b * half + rank_d * wide) // (8 * LANES)
-    grad_tiles += -grad_tiles % owners
+    grad_tiles = (pairs // 2 * channels + rank_d * rank_b * half + rank_d * wide) // (STEP * LANES)
+    grad_tiles += -grad_tiles % planes
     sub = STEP
     subs = chan // sub
     slots = min(SLOTS, 2 * subs)
@@ -888,8 +923,7 @@
         chunk = count // planes
         return [
             pltpu.VMEM((*lead, planes - 1, chunk, *shape), dtype),
-            pltpu.VMEM((*lead, stacks - 1, chunk // stacks, *shape), dtype),
-            pltpu.VMEM((*lead, chunk, *shape), dtype),
+            pltpu.VMEM((*lead, stacks, chunk, *shape), dtype),
         ]
 
     tile = (rank_a, modes_y)
@@ -932,14 +966,14 @@
         pltpu.VMEM((2, tiles, *tile), BF16),
         *reduce_buffers(tiles // parts, tile, BF16, (parts,)),
         pltpu.VMEM((pairs // 2, both), F32),
-        pltpu.VMEM((grad_tiles, 8, LANES), F32),
-        pltpu.VMEM((2, grad_tiles, 8, LANES), F32),
-        *reduce_buffers(grad_tiles, (8, LANES), F32),
+        pltpu.VMEM((grad_tiles, STEP, LANES), BF16),
+        pltpu.VMEM((2, grad_tiles, STEP, LANES), BF16),
+        *reduce_buffers(grad_tiles, (STEP, LANES), BF16),
         pltpu.VMEM((2, rank_a, channels), F32),
         pltpu.VMEM((planes, rank_a, channels), F32),
         pltpu.VMEM((stacks, rank_a, channels), F32),
         *[pltpu.SemaphoreType.DMA((parts, 4, peers))] * 4,
-        *[pltpu.SemaphoreType.DMA((4, peers))] * 2,
+        *[pltpu.SemaphoreType.DMA((3, peers))] * 2,
         *[pltpu.SemaphoreType.DMA((5 + parts,))] * 2,
         *[pltpu.SemaphoreType.DMA((blocks,))] * 2,
         *[pltpu.SemaphoreType.DMA((groups,))] * 2,

time: 95.1 us -> 92.6 us (0.974)
  Pallas kernels: 94.3 us -> 91.8 us
    pallas_call x1, Pallas kernels: 79.4 us -> 76.9 us  [local(): pl.pallas_call(spectral_kernel, in_specs=[anywhere] * 4 + [vmem] * 4, out...]
where the time goes in v4:
time: 92.6 us; the launch traced here: 92.4 us
  Pallas kernels  91.8 us (99%)
    pallas_call x1, Pallas kernels, local(): pl.pallas_call(spectral_kernel, in_specs=[anywhere] * 4 + [vmem] * 4, out...  76.9 us
    pallas_call x1, Pallas kernels, local(): pl.pallas_call(output_kernel, in_specs=[anywhere] * 8, out_specs=[anywher...  14.9 us

profile of v4, /device:TPU:0, one launch (start us, length us, event | category | flops | bytes accessed | tf_op | source)
XLA Modules:
  0.0 92.4 jit_solution(14785655305761328802)
XLA Ops:
  0.6 76.9 %spectral.1 = (bf16[64,128,256]{2,1,0:T(8,128)(2,1)}, bf16[16,128,1024]{2,1,0:T(8,128)(2,1)}, bf16[1024,256]{1,0:T(8,128)(2,1)}, f32[16,256]{1,0:T(8,128)}, f32[...) custom-call(bf16[64,128,1024]{2,1,0:T(8,128)(2,1)} %field.1, bf16[64,128,1024]{2,1,0:T(8,128)(2,1)} %cot.1, ...), custom_call_target="tpu_custom_call" | custom-call | tf_op jit(solution)/shard_map/spectral/pallas_call | solution.py:987
  77.6 14.9 %output.1 = (bf16[64,128,1024]{2,1,0:T(8,128)(2,1)}, bf16[64,128,1024]{2,1,0:T(8,128)(2,1)}, f32[16,256]{1,0:T(8,128)}, f32[256,256]{1,0:T(8,128)}, f32[16,16,128]{2,1,0:T(8,128)}, /*index=5*/f32[2,16,128]{2,1,0:T(8,128)}) custom-call(bf16[256,1024]{1,0:T(8,128)(2,1)} %constant.7.clone.table_in, bf16[64,128,256]{2,1,0:T(8,128)(2,1)} %get-tuple-element.19.rows_in, ...), custom_call_target="tpu_custom_call" | custom-call | tf_op jit(solution)/shard_map/output/pallas_call | solution.py:1013

commit v5 on v4

--- a/solution.py
+++ b/solution.py
@@ -644,16 +644,16 @@
     lax.fori_loop(0, groups, out_body, 0)
     last_lg.plane_back_wait()
     back_copy(parts - 1).start()
+    share = half // parts
     for p in range(parts):
         back_copy(p).wait()
-    for q in range(2):
         for h in range(2):
-            got = lg_all[h].reshape(half, 2, ra, my)[:, q].astype(F32)
-            turned = jnp.swapaxes(got, 0, 1).astype(BF16)
-            for a in range(ra):
-                back_in[
-                    q * mx + h * half : q * mx + (h + 1) * half, a * my : (a + 1) * my
-                ] = turned[a]
+            got = lg_all[h, p * 2 * share : (p + 1) * 2 * share].reshape(share, 2, ra, my)
+            for q in range(2):
+                turned = jnp.swapaxes(got[:, q].astype(F32), 0, 1).astype(BF16)
+                row = q * mx + h * half + p * share
+                for a in range(ra):
+                    back_in[row : row + share, a * my : (a + 1) * my] = turned[a]
     r = dot(csb[...], back_in[...]).astype(BF16)
     for a in range(ra):
         for q in range(2):

time: 92.6 us -> 92.2 us (level)
  no operation moved by 1% of the time
where the time goes in v5:
time: 92.2 us; the launch traced here: 92.1 us
  Pallas kernels  91.4 us (99%)
    pallas_call x1, Pallas kernels, local(): pl.pallas_call(spectral_kernel, in_specs=[anywhere] * 4 + [vmem] * 4, out...  76.6 us
    pallas_call x1, Pallas kernels, local(): pl.pallas_call(output_kernel, in_specs=[anywhere] * 8, out_specs=[anywher...  14.9 us

profile of v5, /device:TPU:0, one launch (start us, length us, event | category | flops | bytes accessed | tf_op | source)
XLA Modules:
  0.0 92.1 jit_solution(6360732839518521874)
XLA Ops:
  0.6 76.6 %spectral.1 = (bf16[64,128,256]{2,1,0:T(8,128)(2,1)}, bf16[16,128,1024]{2,1,0:T(8,128)(2,1)}, bf16[1024,256]{1,0:T(8,128)(2,1)}, f32[16,256]{1,0:T(8,128)}, f32[...) custom-call(bf16[64,128,1024]{2,1,0:T(8,128)(2,1)} %field.1, bf16[64,128,1024]{2,1,0:T(8,128)(2,1)} %cot.1, ...), custom_call_target="tpu_custom_call" | custom-call | tf_op jit(solution)/shard_map/spectral/pallas_call | solution.py:987
  77.2 14.9 %output.1 = (bf16[64,128,1024]{2,1,0:T(8,128)(2,1)}, bf16[64,128,1024]{2,1,0:T(8,128)(2,1)}, f32[16,256]{1,0:T(8,128)}, f32[256,256]{1,0:T(8,128)}, f32[16,16,128]{2,1,0:T(8,128)}, /*index=5*/f32[2,16,128]{2,1,0:T(8,128)}) custom-call(bf16[256,1024]{1,0:T(8,128)(2,1)} %constant.7.clone.table_in, bf16[64,128,256]{2,1,0:T(8,128)(2,1)} %get-tuple-element.19.rows_in, ...), custom_call_target="tpu_custom_call" | custom-call | tf_op jit(solution)/shard_map/output/pallas_call | solution.py:1013
